TPU v7x, 256 devices: a whole 4x4x8 slice. The times are simulated.
256 devices in a mesh: rows: 16 (over x, y), pts: 16 (over z, core).
Axes of the slice: x: 4, y: 4, z: 8, core: 2. Of those that a mesh axis runs over, the one named last changes fastest.
Arguments:
- env_desc: bfloat16 [8192, 1024], P('rows', 'pts'), may hold values from -6 to 6
- point_desc: bfloat16 [16384, 1024], P('pts', 'rows'), may hold values from -6 to 6
- pool_index: int32 [4096, 4], P('rows'), may hold values from 0 to 511
- pool_count: int32 [4096], P('rows'), may hold values from 1 to 4
- pool_weight: float32 [4096, 4], P('rows'), may hold values from -3 to 3
- row_dest: int32 [4096], P('rows'), may hold values from -1 to 2047, as said below
Outputs:
- design: float32 [2048, 16384], P('rows', 'pts')
- gram: float32 [16384, 16384], P('rows', 'pts')
Inputs may be any that keep to these rules, and one draw needn't show every extreme that they name: Slot s pools environments (s // 256) * 512 + pool_index[s, j] of its own structure group. Slot s pools its first pool_count[s] entries. `row_dest`: -1 marks an empty slot; every row 0 .. 2047 is named by exactly one slot; the slots of one structure group (aligned blocks of 256 slots) name at most 16 rows of any aligned block of 128 rows, and in every draw some structure group names exactly 16 rows of every such block.
All inputs are finite; a program needn't handle non-finite values.
Results may differ from a plain program's by a relative error of at most 0.0003.
Values may be sent and summed in bfloat16 or wider, within the bound.
A program may use at most 128 MiB of HBM per device.

v0:
```python
import jax
import jax.numpy as jnp
from jax import lax
from jax.sharding import PartitionSpec as P

damping = 0.5


def from_root(value, axis, source):
    kept = jnp.where(lax.axis_index(axis) == source, value, 0).astype(value.dtype)
    return lax.psum(kept, axis)


def kernel_values(left, right):
    products = lax.dot_general(
        left, right, (((1,), (1,)), ((), ())), preferred_element_type=jnp.float32
    )
    scaled = products * left.shape[1] ** (-0.5)
    squared = scaled * scaled
    return 0.25 * squared * squared


def live_weights(pool_count, pool_weight):
    members = jnp.arange(pool_weight.shape[1], dtype=jnp.int32)
    return jnp.where(members[None, :] < pool_count[:, None], pool_weight, 0.0)


def pool_rows(kernel_table, env_index, weights_live):
    pooled = jnp.zeros((env_index.shape[0], kernel_table.shape[1]), jnp.float32)
    for member in range(env_index.shape[1]):
        pooled = pooled + weights_live[:, member : member + 1] * kernel_table[env_index[:, member]]
    return pooled


def on_device(env_desc, point_desc, pool_index, pool_count, pool_weight, row_dest):
    groups = lax.axis_size("rows")
    slot_total = pool_index.shape[0]
    balanced = slot_total // 2
    slot_share = slot_total // groups
    points = lax.all_gather(point_desc, "rows", axis=1, tiled=True)
    width_pts = points.shape[0]
    weights_live = live_weights(pool_count, pool_weight)
    live_slot = row_dest >= 0
    owner_group = jnp.where(live_slot, row_dest // balanced, groups)
    within = jnp.where(live_slot, row_dest % balanced, balanced)
    owner_table = (owner_group[:, None] == jnp.arange(groups, dtype=jnp.int32)[None, :]).astype(
        jnp.int32
    )
    earlier = jnp.cumsum(owner_table, axis=0) - owner_table
    slot_rank = jnp.sum(earlier * owner_table, axis=1)
    outbox_place = (
        jnp.full((groups, slot_share), balanced, jnp.int32)
        .at[owner_group, slot_rank]
        .set(within, mode="drop")
    )
    features = lax.all_gather(env_desc, "pts", axis=1, tiled=True)
    slot_rows = pool_rows(kernel_values(features, points), pool_index, weights_live)
    outbox = (
        jnp.zeros((groups, slot_share, width_pts), jnp.float32)
        .at[owner_group, slot_rank]
        .set(slot_rows, mode="drop")
    )
    inbox_rows, inbox_place = (
        lax.all_to_all(outbox, "rows", split_axis=0, concat_axis=0, tiled=True),
        lax.all_to_all(outbox_place, "rows", split_axis=0, concat_axis=0, tiled=True),
    )
    design = (
        jnp.zeros((balanced, width_pts), jnp.float32)
        .at[inbox_place.reshape(-1)]
        .set(inbox_rows.reshape(-1, width_pts), mode="drop")
    )
    all_rows = lax.all_gather(design, "rows", axis=0, tiled=True)
    per_group = lax.axis_size("pts") // groups
    row_group = lax.axis_index("rows")
    diagonal_panel = from_root(all_rows, "pts", row_group * per_group + 0)
    pieces = lax.dot_general(
        diagonal_panel,
        all_rows,
        (((0,), (0,)), ((), ())),
        precision=lax.Precision.HIGHEST,
        preferred_element_type=jnp.float32,
    )
    gram_tile = pieces * (1.0 / all_rows.shape[0])
    tile_rows = gram_tile.shape[0]
    row_ids = row_group * tile_rows + jnp.arange(tile_rows, dtype=jnp.int32)
    col_ids = lax.axis_index("pts") * width_pts + jnp.arange(width_pts, dtype=jnp.int32)
    gram_tile = gram_tile + jnp.where(row_ids[:, None] == col_ids[None, :], damping, 0.0)
    return (design, gram_tile)


def solution(mesh):
    in_specs = (
        P("rows", "pts"),
        P("pts", "rows"),
        P("rows", None),
        P("rows"),
        P("rows", None),
        P("rows"),
    )
    out_specs = (P("rows", "pts"), P("rows", "pts"))
    return jax.shard_map(
        on_device, mesh=mesh, in_specs=in_specs, out_specs=out_specs, check_vma=False
    )
```

profile of v0, /device:TPU:35, one launch (start us, length us, event | category | flops | bytes accessed | tf_op | source)
XLA Modules:
  0.0 427.6 jit_solution(4410987133742169312)
XLA Ops:
  7.2 0.7 all-gather.4.cloned.1.call-update
  7.9 0.7 all-gather.6.cloned.1.call-update
  8.6 0.7 compare_select_fusion.6
  10.9 36.7 %scatter_fusion = s32[16,16]{1,0:T(8,128)} fusion(s32[16,16]{1,0:T(8,128)} %broadcast_in_dim.50, s32[256]{0:T(256)S(1)} %bitcast.40, s32[256]{0:T(256)S(1)} %get-tuple-element.12), kind=kCustom, calls=%fused_computation.4 | custom fusion | bytes 5120 | tf_op jit(solution)/shard_map/scatter | solution.py:54
  47.6 7.1 %all-to-all-start = ((s32[16,1,16]{2,1,0:T(1,128)}), s32[16,1,16]{2,1,0:T(1,128)S(1)}, u32[]{:S(2)}, u32[]{:S(2)}) async-start(s32[16,1,16]{2,1,0:T(1,128)} %bitcast.6), calls=%async_computation | async-start | bytes 16384 | tf_op jit(solution)/shard_map/all_to_all | solution.py:65
  54.7 0.8 compare_select_fusion.3
  55.6 0.7 fusion.6
  56.4 43.7 %all-gather.6.cloned.1.call-done = bf16[1024,1024]{0,1:T(8,128)(2,1)} async-done(((bf16[1024,64]{0,1:T(8,128)(2,1)}), bf16[1024,1024]{0,1:T(8,128)(2,1)}) %all-gather.6.cloned.1.call-update) | async-done | bytes 2097168 | tf_op jit(solution)/shard_map/all_gather | solution.py:40
  100.0 3.2 multiply_multiply_fusion
  103.2 1.1 gather_fusion
  104.3 2.1 gather_fusion.1
  106.4 2.0 gather_fusion.2
  108.4 2.0 gather_fusion.3
  110.4 2.2 multiply_add_fusion
  112.6 1.1 broadcast_in_dim.54
  113.7 37.6 %scatter_fusion.1 = f32[16,16,1024]{2,1,0:T(8,128)} fusion(f32[16,16,1024]{2,1,0:T(8,128)} %broadcast_in_dim.54, s32[256]{0:T(256)S(1)} %bitcast.41, f32[256,1024]{1,0:T(8,128)S(1)} %multiply_add_fusion), kind=kCustom, calls=%fused_computation.5 | custom fusion | bytes 3147776 | tf_op jit(solution)/shard_map/scatter | solution.py:61
  151.3 4.9 %all-to-all-start.1 = ((f32[16,16,1024]{2,1,0:T(8,128)}), f32[16,16,1024]{2,1,0:T(8,128)S(1)}, u32[]{:S(2)}, u32[]{:S(2)}) async-start(f32[16,16,1024]{2,1,0:T(8,128)} %scatter_fusion.1), calls=%async_computation.1 | async-start | bytes 2097152 | tf_op jit(solution)/shard_map/all_to_all | solution.py:64
  156.8 0.7 reduce.5
  157.6 11.5 %all-to-all-done.1 = f32[16,16,1024]{2,1,0:T(8,128)S(1)} async-done(((f32[16,16,1024]{2,1,0:T(8,128)}), f32[16,16,1024]{2,1,0:T(8,128)S(1)}, u32[]{:S(2)}, u32[]{:S(2)}) %all-to-all-start.1) | async-done | bytes 1048608 | tf_op jit(solution)/shard_map/all_to_all | solution.py:64
  169.1 2.2 scatter_custom_fusion.2
  171.6 78.0 %all-gather.8.cloned.1.call-done = f32[2048,1024]{1,0:T(8,128)} async-done(((f32[128,1024]{1,0:T(8,128)}), f32[2048,1024]{1,0:T(8,128)}) %all-gather.8.cloned.1.call-update) | async-done | bytes 8388624 | tf_op jit(solution)/shard_map/all_gather | solution.py:72
  249.6 5.1 %broadcast_select_fusion = f32[2048,1024]{1,0:T(8,128)} fusion(f32[2048,1024]{1,0:T(8,128)} %all-gather.8.cloned.1.call-done, pred[]{:T(512)S(6)} %eq.48), kind=kLoop, calls=%fused_computation.8 | loop fusion | flops 2097152 | bytes 16777216 | tf_op jit(solution)/shard_map/jit(_where)/select_n | solution.py:10
  254.7 134.4 %all-reduce.2.cloned.1.call-done = f32[2048,1024]{1,0:T(8,128)} async-done(((f32[2048,1024]{1,0:T(8,128)}), f32[2048,1024]{1,0:T(8,128)}) %all-reduce.2.cloned.1.call-update) | async-done | bytes 8388624 | tf_op jit(solution)/shard_map/psum | solution.py:11
  389.1 32.0 %select_add_fusion = f32[1024,1024]{1,0:T(8,128)} fusion(f32[2048,1024]{1,0:T(8,128)} %all-reduce.2.cloned.1.call-done, f32[2048,1024]{1,0:T(8,128)} %all-gather.8.cloned.1.call-done, s32[1024]{0:T(1024)S(1)} %get-tuple-element.13, s32[1024]{0:T(1024)S(1)} %get-tuple-element.14), kind=kOutput, calls=%fused_computation.7 | convolution fusion | flops 25773998080 | bytes 20979712 | tf_op jit(solution)/shard_map/dot_general | solution.py:76
  (25 shorter events, 2.5 us)
Async XLA Ops:
  7.2 49.2 %all-gather.4.cloned.1.call-start = ((), (), s32[]{:S(2)}) async-start(), calls=%async_computation.2 | async-start | bytes 1114112 | tf_op jit(solution)/shard_map/all_gather | solution.py:56
  7.9 92.1 %all-gather.6.cloned.1.call-start = ((), (), s32[]{:S(2)}) async-start(), calls=%async_computation.3 | async-start | bytes 2228224 | tf_op jit(solution)/shard_map/all_gather | solution.py:40
  47.6 103.7 %all-to-all-start = ((s32[16,1,16]{2,1,0:T(1,128)}), s32[16,1,16]{2,1,0:T(1,128)S(1)}, u32[]{:S(2)}, u32[]{:S(2)}) async-start(s32[16,1,16]{2,1,0:T(1,128)} %bitcast.6), calls=%async_computation | async-start | bytes 16384 | tf_op jit(solution)/shard_map/all_to_all | solution.py:65
  151.3 17.8 %all-to-all-start.1 = ((f32[16,16,1024]{2,1,0:T(8,128)}), f32[16,16,1024]{2,1,0:T(8,128)S(1)}, u32[]{:S(2)}, u32[]{:S(2)}) async-start(f32[16,16,1024]{2,1,0:T(8,128)} %scatter_fusion.1), calls=%async_computation.1 | async-start | bytes 2097152 | tf_op jit(solution)/shard_map/all_to_all | solution.py:64
  156.3 93.3 %all-gather.8.cloned.1.call-start = ((), (), s32[]{:S(2)}) async-start(), calls=%async_computation.4 | async-start | bytes 8912896 | tf_op jit(solution)/shard_map/all_gather | solution.py:72
  171.3 217.8 %all-reduce.2.cloned.1.call-start = ((), (), s32[]{:S(2)}) async-start(), calls=%async_computation.5 | async-start | bytes 16777216 | tf_op jit(solution)/shard_map/psum | solution.py:11
Sparse Core Ops, SparseCore 0:
  9.8 40.8 all-gather.3
  53.2 46.8 all-gather.5
  171.5 78.0 all-gather.7
  254.8 134.2 all-reduce.1
where the time goes:
time: 434 us; the launch traced here: 428 us
  waiting for transfers between devices  269 us (62%)
  local copies, waits for them, and re-layouts  86.2 us (20%)
  matrix products  35.2 us (8%)
  between operations  13.9 us (3%)
  starting transfers between devices  12.4 us (3%)
  other arithmetic  11 us (3%)
    psum x1, waiting for transfers between devices, from_root(): return lax.psum(kept, axis)  134 us
    all_gather x1, waiting for transfers between devices, on_device(): all_rows = lax.all_gather(design, 'rows', axis=0, tiled=True)  78 us
    all_gather x1, waiting for transfers between devices, on_device(): points = lax.all_gather(point_desc, 'rows', axis=1, tiled=True)  43.7 us
    scatter x1, local copies, waits for them, and re-layouts, on_device(): outbox = jnp.zeros((groups, slot_share, width_pts), jnp.float32).at[owner...  37.6 us
    scatter x1, local copies, waits for them, and re-layouts, on_device(): outbox_place = jnp.full((groups, slot_share), balanced, jnp.int32).at[own...  36.7 us
    dot_general x1, matrix products, on_device(): lax.dot_general(diagonal_panel, all_rows, (((0,), (0,)), ((), ())), preci...  32 us
    all_to_all x1, waiting for transfers between devices, on_device(): lax.all_to_all(outbox, 'rows', split_axis=0, concat_axis=0, tiled=True)  11.5 us
  transfers between devices with their start and end apart: 6, of which 4 were waited for; matrix products, arithmetic and copies ran while one was open for 22% of the time, Pallas kernels for 0%

commit v1 on v0

v1 whole, which is shorter than its diff:
```python
import jax
import jax.numpy as jnp
from jax import lax
from jax.experimental import pallas as pl
from jax.experimental.pallas import tpu as pltpu
from jax.sharding import PartitionSpec as P

damping = 0.5
MESH = pl.DeviceIdType.MESH
f32, bf16, i16 = jnp.float32, jnp.bfloat16, jnp.int16
HALF = 528
CUT = 256
VMEM = pltpu.VMEM


def split_bf16(value):
    high = value.astype(bf16)
    return high, (value - high.astype(f32)).astype(bf16)


def where_am_i():
    r = lax.axis_index("rows")
    p = lax.axis_index("pts")
    return r // 4, r % 4, p // 2, p % 2


def plane_id(x, y, dx, dy):
    return ((x + dx + 4) % 4) * 4 + (y + dy + 4) % 4


def gather_keys():
    keys = []
    for half in (0, 1):
        for i in (0, 1, -1, 2):
            for j in (0, 1, -1, 2):
                if (i, j) == (0, 0):
                    continue
                two = j == 2 or (j == 0 and i == 2)
                keys += [(half, i, j, q) for q in ((0, 1) if two else (None,))]
    return {key: n for n, key in enumerate(keys)}


KEYS = gather_keys()


class TorusGather:
    def __init__(self, x, y, own, view, send_sems, recv_sems):
        self.x, self.y, self.own, self.view = x, y, own, view
        self.send_sems, self.recv_sems = send_sems, recv_sems
        self.sends = 0

    def offset(self, half, a, b):
        return (a, b) if half == 0 else (b, a)

    def block(self, half, i, j):
        return plane_id(self.x, self.y, *self.offset(half, i, j))

    def copy(self, half, i, j, q, to, key):
        target = plane_id(self.x, self.y, *self.offset(half, *to))
        block = self.block(half, i, j)
        src = self.own(half, q) if (i, j) == (0, 0) else self.view(block, half, q)
        pltpu.make_async_remote_copy(
            src_ref=src,
            dst_ref=self.view(block, half, q),
            send_sem=self.send_sems.at[self.sends],
            recv_sem=self.recv_sems.at[KEYS[key]],
            device_id={"rows": target},
            device_id_type=MESH,
        ).start()
        self.sends += 1

    def wait(self, half, i, j, q):
        ref = self.view(self.block(half, i, j), half, q)
        pltpu.make_async_copy(ref, ref, self.recv_sems.at[KEYS[(half, i, j, q)]]).wait()

    def start(self):
        for half in (0, 1):
            for d in (1, -1):
                self.copy(half, 0, 0, None, (d, 0), (half, -d, 0, None))
        for half in (0, 1):
            for d in (1, -1):
                self.copy(half, 0, 0, None, (0, d), (half, 0, -d, None))

    def first(self):
        for half in (0, 1):
            for d in (1, -1):
                q = 0 if d == 1 else 1
                self.wait(half, -d, 0, None)
                self.copy(half, -d, 0, q, (d, 0), (half, 2, 0, q))
                for e in (1, -1):
                    self.copy(half, -d, 0, None, (0, e), (half, -d, -e, None))

    def across(self, i):
        for half in (0, 1):
            for d in (1, -1):
                q = 0 if d == 1 else 1
                self.wait(half, i, -d, None)
                self.copy(half, i, -d, q, (0, d), (half, i, 2, q))

    def far(self):
        for half in (0, 1):
            for q in (0, 1):
                self.wait(half, 2, 0, q)
            for e in (1, -1):
                self.copy(half, 2, 0, None, (0, e), (half, 2, -e, None))

    def last(self, i):
        for half in (0, 1):
            for q in (0, 1):
                self.wait(half, i, 2, q)

    def drain(self):
        n = 0
        for whole in self.order():
            ref = self.own(0, whole)
            pltpu.make_async_copy(ref, ref, self.send_sems.at[n]).wait()
            n += 1

    def order(self):
        sizes = [None] * 8
        for half in (0, 1):
            for d in (1, -1):
                sizes += [0 if d == 1 else 1, None, None]
        sizes += [0, 1] * 2
        sizes += [None] * 4
        sizes += [0, 1] * 2
        sizes += [0, 1] * 2
        sizes += [0, 1] * 2
        return sizes


ORDER = [(0, 0), (1, 0), (-1, 0), (0, 1), (0, -1), (1, 1), (1, -1), (-1, 1), (-1, -1),
         (0, 2), (2, 0), (1, 2), (-1, 2), (2, 1), (2, -1), (2, 2)]
LAG = 2
PAIRS = 8
READY = 6


def block_of(x, y, n):
    dx = jnp.int32(0)
    dy = jnp.int32(0)
    for k, (a, b) in enumerate(ORDER):
        hit = (n == k).astype(jnp.int32)
        dx = dx + hit * (a + 4)
        dy = dy + hit * (b + 4)
    return ((x + dx) % 4) * 4 + (y + dy) % 4


def column_scale(tile, factor):
    parts = tile.astype(jnp.int32).astype(f32)
    return jnp.exp2(parts[:8]) * (parts[8:] * (factor / 32767.0))


def as_i16(value):
    return jnp.clip(jnp.round(value), -32767.0, 32767.0).astype(jnp.int32).astype(i16)


def gram_kernel(enc_ref, out_ref, buf, hp, lp, hrt, lrt, sends, recvs, zsends, zrecvs, own_sem):
    x, y, z, c = where_am_i()
    r = x * 4 + y
    z0, c0 = r // 2, r % 2
    dz = (z - z0 + 8) % 8
    root_chip = dz == 0
    root = jnp.logical_and(root_chip, c == c0)
    up = {"pts": ((z + 1) % 8) * 2}
    down = {"pts": ((z + 7) % 8) * 2 + 1}
    other = {"pts": z * 2 + 1 - c}
    barrier = pltpu.get_barrier_semaphore()
    for dx, dy in ((1, 0), (-1, 0), (0, 1), (0, -1)):
        pl.semaphore_signal(barrier, inc=1, device_id={"rows": plane_id(x, y, dx, dy)}, device_id_type=MESH)
    for dc in (0, 1):
        for target in ((z + 1) % 8, (z + 7) % 8):
            pl.semaphore_signal(barrier, inc=1, device_id={"pts": target * 2 + dc}, device_id_type=MESH)
    pl.semaphore_signal(barrier, inc=1, device_id=other, device_id_type=MESH)
    pl.semaphore_wait(barrier, 9)

    def cut(ref, q):
        if q is None:
            return ref
        return ref.at[pl.ds(0, CUT)] if q == 0 else ref.at[pl.ds(CUT, HALF - CUT)]

    gather = TorusGather(
        x, y,
        lambda half, q: cut(enc_ref.at[half], q),
        lambda block, half, q: cut(buf.at[0, block, half], q),
        sends, recvs,
    )
    gather.start()
    own_copy = pltpu.make_async_copy(enc_ref, buf.at[0, r], own_sem)
    own_copy.start()

    rows = r * 1024 + lax.broadcasted_iota(jnp.int32, (128, 1024), 0)
    cols = (z * 2 + c) * 1024 + lax.broadcasted_iota(jnp.int32, (128, 1024), 1)

    @pl.loop(0, 8)
    def _(m):
        out_ref[pl.ds(pl.multiple_of(m * 128, 128), 128), :] = jnp.where(rows + m * 128 == cols, damping, 0.0).astype(f32)

    own_copy.wait()
    gather.first()
    gather.across(0)
    gather.far()
    gather.across(1)
    gather.across(-1)
    gather.across(2)
    for i in (0, 1, -1, 2):
        gather.last(i)

    def z_copy(block, half, target, n, k):
        return pltpu.make_async_remote_copy(
            src_ref=buf.at[jnp.where(root, 0, 1), block, half],
            dst_ref=buf.at[1, block, half],
            send_sem=zsends.at[n, k],
            recv_sem=zrecvs.at[n, half],
            device_id=target,
            device_id_type=MESH,
        )

    def z_wait(block, half, n):
        ref = buf.at[1, block, half]
        pltpu.make_async_copy(ref, ref, zrecvs.at[n, half]).wait()

    hops = jnp.where(c == 0, dz, (8 - dz) % 8)
    not_end = jnp.where(c == 0, dz != 7, dz != 1)

    def pass_on(n):
        block = block_of(x, y, n)

        @pl.when(root)
        def _():
            z_copy(block, 0, up, n, 0).start()
            z_copy(block, 1, down, n, 1).start()
            z_copy(block, 0, other, n, 2).start()
            z_copy(block, 1, other, n, 3).start()

        for half in (0, 1):
            @pl.when(jnp.logical_and(jnp.logical_not(root_chip), c == half))
            def _():
                z_wait(block, half, n)

                @pl.when(not_end)
                def _():
                    z_copy(block, half, up if half == 0 else down, n, 0).start()

                z_copy(block, half, other, n, 1).start()

    def drained(n):
        ref = buf.at[0, 0, 0]

        @pl.when(root)
        def _():
            for k in range(4):
                pltpu.make_async_copy(ref, ref, zsends.at[n, k]).wait()

        @pl.when(jnp.logical_not(root_chip))
        def _():
            @pl.when(not_end)
            def _():
                pltpu.make_async_copy(ref, ref, zsends.at[n, 0]).wait()

            pltpu.make_async_copy(ref, ref, zsends.at[n, 1]).wait()

    from_root = jnp.where(root, 0, 1)

    def decode(n, place):
        block = block_of(x, y, n)
        for half in (0, 1):
            @pl.when(jnp.logical_and(jnp.logical_not(root), jnp.logical_or(root_chip, c != half)))
            def _():
                z_wait(block, half, n)

        scale_p = column_scale(buf[0, block, 0, pl.ds(512, 16), :], 2.0 ** -11)
        scale_r = column_scale(buf[from_root, block, 0, pl.ds(512, 16), :], 1.0)
        for j in range(8):
            cols = slice(128 * j, 128 * j + 128)
            for half in (0, 1):
                part = buf[0, block, half, pl.ds(64 * j, 64), :].astype(jnp.int32).astype(f32) * scale_p[j : j + 1, :]
                high, low = split_bf16(part)
                spot = pl.ds(place * 128 + half * 64, 64)
                hp[spot, cols] = high
                lp[spot, cols] = low
            both = jnp.concatenate(
                [buf[from_root, block, half, pl.ds(64 * j, 64), :].astype(jnp.int32).astype(f32) for half in (0, 1)], axis=0
            )
            high, low = split_bf16((both * scale_r[j : j + 1, :]).T)
            hrt[cols, pl.ds(place * 128, 128)] = high
            lrt[cols, pl.ds(place * 128, 128)] = low

    def multiply():
        right = jnp.concatenate([hp[...], lp[...], hp[...]], axis=0)

        @pl.loop(0, 4)
        def _(m):
            spot = pl.ds(pl.multiple_of(m * 256, 256), 256)
            high = hrt[spot, :]
            left = jnp.concatenate([high, high, lrt[spot, :]], axis=1)
            out_ref[spot, :] += jnp.dot(left, right, preferred_element_type=f32)

    far_hops = jnp.maximum(hops, (8 - hops) % 8)

    @pl.loop(0, 16 + 8 * LAG + 2)
    def _(s):
        n = s - hops * LAG

        @pl.when(jnp.logical_and(n >= 0, n < 16))
        def _():
            pass_on(n)

        m = s - far_hops * LAG - 1

        @pl.when(jnp.logical_and(jnp.logical_and(m >= 0, m < 16), m % 2 == 1))
        def _():
            decode(m - 1, 0)
            decode(m, 1)
            multiply()

    gather.drain()

    @pl.loop(0, 16)
    def _(n):
        drained(n)


def gram_of(enc):
    return pl.pallas_call(
        gram_kernel,
        out_shape=jax.ShapeDtypeStruct((1024, 1024), f32),
        in_specs=[pl.BlockSpec(memory_space=VMEM)],
        out_specs=pl.BlockSpec(memory_space=VMEM),
        scratch_shapes=[
            VMEM((2, 16, 2, HALF, 128), i16),
            VMEM((256, 1024), bf16),
            VMEM((256, 1024), bf16),
            VMEM((1024, 256), bf16),
            VMEM((1024, 256), bf16),
            pltpu.SemaphoreType.DMA((40,)),
            pltpu.SemaphoreType.DMA((40,)),
            pltpu.SemaphoreType.DMA((16, 4)),
            pltpu.SemaphoreType.DMA((16, 2)),
            pltpu.SemaphoreType.DMA(()),
        ],
        compiler_params=pltpu.CompilerParams(collective_id=1, has_side_effects=True, vmem_limit_bytes=56 << 20),
        name="gram",
    )(enc)


def design_kernel(feat_ref, meta_ref, points_ref, design_ref, enc_ref, lhs):
    lane = lax.broadcasted_iota(jnp.int32, (128, 128), 1)
    for k in range(8):
        for pair in (0, 1):
            a = feat_ref[2 * k, pair].astype(f32)
            b = feat_ref[2 * k + 1, pair].astype(f32)
            even = jnp.where(lane < 64, a, pltpu.roll(b, 64, 1))
            odd = jnp.where(lane < 64, pltpu.roll(a, 64, 1), b)
            lhs[pl.ds(pair * 256, 128), pl.ds(k * 128, 128)] = even.astype(bf16)
            lhs[pl.ds(pair * 256 + 128, 128), pl.ds(k * 128, 128)] = odd.astype(bf16)
    meta = meta_ref[...]
    weights = [meta[:, j : j + 1] + meta[:, j + 4 : j + 5] + meta[:, j + 8 : j + 9] for j in range(4)]
    tops, bottoms = [], []
    for t in range(4):
        cols = pl.ds(t * 256, 256)
        products = jnp.dot(lhs[...], points_ref[:, cols], preferred_element_type=f32)
        scaled = products * (1.0 / 32.0)
        squared = scaled * scaled
        values = 0.25 * squared * squared
        rows = jnp.zeros((128, 256), f32)
        for j in range(4):
            rows = rows + weights[j] * values[j * 128 : (j + 1) * 128]
        design_ref[:, cols] = rows
        largest = jnp.maximum(jnp.max(jnp.abs(rows), axis=0, keepdims=True), 1e-30)
        exponent = jnp.floor(jnp.log2(largest)) - 14.0
        mantissa = jnp.minimum(jnp.ceil(largest * jnp.exp2(-exponent)), 32767.0)
        coded = rows * (32767.0 / (mantissa * jnp.exp2(exponent)))
        for u in range(2):
            j = 2 * t + u
            part = coded[:, 128 * u : 128 * u + 128]
            enc_ref[0, pl.ds(64 * j, 64), :] = as_i16(part[:64])
            enc_ref[1, pl.ds(64 * j, 64), :] = as_i16(part[64:])
            tops.append(exponent[:, 128 * u : 128 * u + 128])
            bottoms.append(mantissa[:, 128 * u : 128 * u + 128])
    tile = as_i16(jnp.concatenate(tops + bottoms, axis=0))
    enc_ref[0, pl.ds(512, 16), :] = tile
    enc_ref[1, pl.ds(512, 16), :] = tile


def design_of(feat, meta, points):
    return pl.pallas_call(
        design_kernel,
        out_shape=(jax.ShapeDtypeStruct((128, 1024), f32), jax.ShapeDtypeStruct((2, HALF, 128), i16)),
        in_specs=[pl.BlockSpec(memory_space=VMEM)] * 3,
        out_specs=(pl.BlockSpec(memory_space=VMEM), pl.BlockSpec(memory_space=VMEM)),
        scratch_shapes=[VMEM((512, 1024), bf16)],
        name="design",
    )(feat, meta, points)


def outbox_of(env, pool_index, pool_count, pool_weight, row_dest):
    members = jnp.arange(4, dtype=jnp.int32)
    live = row_dest >= 0
    dest = jnp.where(live, row_dest // 128, 16)
    within = jnp.where(live, row_dest % 128 + 1, 0)
    owner = (dest[:, None] == jnp.arange(16, dtype=jnp.int32)[None, :]).astype(f32)
    ids = jnp.arange(256, dtype=jnp.int32)
    earlier = jnp.dot((ids[:, None] > ids[None, :]).astype(f32), owner)
    rank = jnp.sum(earlier * owner, axis=1).astype(jnp.int32)
    place = jnp.where(live, dest * 16 + rank, 256)
    move = (ids[:, None] == place[None, :]).astype(bf16)
    envs = jnp.arange(512, dtype=jnp.int32)
    picked = [
        jnp.dot((pool_index[:, j : j + 1] == envs[None, :]).astype(bf16), env, preferred_element_type=f32).astype(bf16)
        for j in range(4)
    ]
    weight = jnp.where(members[None, :] < pool_count[:, None], pool_weight, 0.0)
    high = lax.reduce_precision(weight, 8, 7)
    mid = lax.reduce_precision(weight - high, 8, 7)
    low = weight - high - mid
    meta = jnp.concatenate([high, mid, low, within[:, None].astype(f32), jnp.zeros((256, 115), f32)], axis=1).astype(bf16)
    everything = jnp.concatenate(picked + [meta], axis=1)
    moved = jnp.dot(move, everything, preferred_element_type=f32).astype(bf16)
    return jnp.concatenate([moved[:, 128 * k : 128 * k + 128].reshape(16, 16, 128) for k in range(3)], axis=1)


def on_device(env_desc, point_desc, pool_index, pool_count, pool_weight, row_dest):
    points = lax.all_gather(point_desc.T, "rows", axis=0, tiled=True)
    outbox = outbox_of(env_desc, pool_index, pool_count, pool_weight, row_dest)
    inbox = lax.all_to_all(outbox, "rows", split_axis=0, concat_axis=0, tiled=True)
    parts = [inbox[:, 16 * k : 16 * k + 16].reshape(256, 128) for k in range(3)]
    spots = parts[2][:, 12:13].astype(f32)
    put = (spots == jnp.arange(1, 129, dtype=f32)[None, :]).astype(bf16)
    placed = [lax.dot_general(put, part, (((0,), (0,)), ((), ())), preferred_element_type=f32) for part in parts]
    mine = jnp.stack([placed[0].astype(bf16), placed[1].astype(bf16)])
    feat = lax.all_gather(mine, "pts", axis=0)
    design, enc = design_of(feat, placed[2], points)
    return design, gram_of(enc)


def solution(mesh):
    in_specs = (
        P("rows", "pts"),
        P("pts", "rows"),
        P("rows", None),
        P("rows"),
        P("rows", None),
        P("rows"),
    )
    out_specs = (P("rows", "pts"), P("rows", "pts"))
    return jax.shard_map(
        on_device, mesh=mesh, in_specs=in_specs, out_specs=out_specs, check_vma=False
    )
```

time: 434 us -> 234 us (0.54); the launches traced: 428 us -> 233 us
  waiting for transfers between devices: 269 us -> 94.2 us
  Pallas kernels: 0 us -> 104 us
  local copies, waits for them, and re-layouts: 86.2 us -> 6.94 us
  matrix products: 35.2 us -> 3.09 us
  other arithmetic: 11 us -> 3.64 us
  starting transfers between devices: 12.4 us -> 7 us
    psum x1 -> x0, waiting for transfers between devices: 134 us -> none  [from_root(): return lax.psum(kept, axis)]
    pallas_call x0 -> x2, Pallas kernels: none -> 104 us  [the longest x1 99.9 us: gram_of(): pl.pallas_call(gram_kernel, out_shape=jax.ShapeDtypeStruct((1024, 1024),...]
    scatter x3 -> x0, local copies, waits for them, and re-layouts: 76.5 us -> none  [the longest x1 37.6 us: on_device(): outbox = jnp.zeros((groups, slot_share, width_pts), jnp.float32).at[owner...]
    all_gather x3 -> x2, waiting for transfers between devices: 122 us -> 87.8 us  [the longest x1 49.3 us: on_device(): points = lax.all_gather(point_desc.T, 'rows', axis=0, tiled=True)]
    dot_general x2 -> x9, matrix products: 35.2 us -> 3.09 us  [the longest x3 1.49 us: on_device(): lax.dot_general(put, part, (((0,), (0,)), ((), ())), preferred_element_ty...]
    gather x4 -> x0, local copies, waits for them, and re-layouts: 7.2 us -> none  [pool_rows(): kernel_table[env_index[:, member]]]
    all_to_all x1 -> x0, starting transfers between devices: 7.09 us -> none  [on_device(): lax.all_to_all(outbox_place, 'rows', split_axis=0, concat_axis=0, tiled=T...]
    select_n x5 -> x2, other arithmetic: 7.37 us -> 1.42 us  [the longest x1 0.72 us: outbox_of(): dest = jnp.where(live, row_dest // 128, 16)]
  transfers between devices with their start and end apart: 6 -> 3, of which waited for: 4 -> 3; matrix products, arithmetic and copies ran while one was open for 22% -> 0% of each run, Pallas kernels for 0% -> 0%
where the time goes in v1:
time: 234 us; the launch traced here: 233 us
  Pallas kernels  104 us (44%)
  waiting for transfers between devices  94.2 us (40%)
  between operations  14.1 us (6%)
  starting transfers between devices  7 us (3%)
  local copies, waits for them, and re-layouts  6.94 us (3%)
  other arithmetic  3.64 us (2%)
  matrix products  3.09 us (1%)
    pallas_call x1, Pallas kernels, gram_of(): pl.pallas_call(gram_kernel, out_shape=jax.ShapeDtypeStruct((1024, 1024),...  99.9 us
    all_gather x1, waiting for transfers between devices, on_device(): points = lax.all_gather(point_desc.T, 'rows', axis=0, tiled=True)  49.3 us
    all_gather x1, waiting for transfers between devices, on_device(): feat = lax.all_gather(mine, 'pts', axis=0)  38.4 us
    all_to_all x1, starting transfers between devices, on_device(): lax.all_to_all(outbox, 'rows', split_axis=0, concat_axis=0, tiled=True)  6.92 us
    all_to_all x1, waiting for transfers between devices, on_device(): lax.all_to_all(outbox, 'rows', split_axis=0, concat_axis=0, tiled=True)  5.74 us
    unnamed x3, local copies, waits for them, and re-layouts  4.8 us
  transfers between devices with their start and end apart: 3, of which 3 were waited for; matrix products, arithmetic and copies ran while one was open for 0% of the time, Pallas kernels for 0%

profile of v1, /device:TPU:35, one launch (start us, length us, event | category | flops | bytes accessed | tf_op | source)
XLA Modules:
  0.0 233.3 jit_solution(16156003386041484231)
XLA Ops:
  7.2 0.7 fusion.23
  7.9 0.2 fusion.2
  8.1 0.7 add_select_fusion
  8.8 0.8 fusion.26
  9.6 0.3 convolution_convert_fusion.5
  9.9 0.3 convolution_convert_fusion.3
  10.5 0.3 convolution_convert_fusion.6
  10.8 0.3 convolution_convert_fusion.4
  11.3 0.7 fusion.19
  12.6 0.2 concatenate.9
  12.8 0.2 convolution_convert_fusion
  13.1 0.7 pad_maximum_fusion
  13.8 6.9 %all-to-all-start = ((bf16[16,48,128]{2,1,0:T(8,128)(2,1)}), bf16[16,48,128]{2,1,0:T(8,128)(2,1)S(1)}, u32[]{:S(2)}, u32[]{:S(2)}) async-start(bf16[16,48,128]{2,1,0:T(8,128)(2,1)} %pad_maximum_fusion), calls=%async_computation | async-start | bytes 393216 | tf_op jit(solution)/shard_map/all_to_all | solution.py:426
  20.8 5.7 %all-to-all-done = bf16[16,48,128]{2,1,0:T(8,128)(2,1)S(1)} async-done(((bf16[16,48,128]{2,1,0:T(8,128)(2,1)}), bf16[16,48,128]{2,1,0:T(8,128)(2,1)S(1)}, u32[]{:S(2)}, u32[]{:S(2)}) %all-to-all-start) | async-done | bytes 196640 | tf_op jit(solution)/shard_map/all_to_all | solution.py:426
  26.7 0.3 fusion.1
  27.0 0.3 fusion
  27.3 0.6 pad_maximum_fusion.1
  28.0 0.7 all-gather.4.cloned.1.call-update
  28.7 0.9 fusion.7.meta_ref
  29.6 38.4 %all-gather.6.cloned.1.call-done = bf16[32,128,128]{2,1,0:T(8,128)(2,1)} async-done(((bf16[2,128,128]{2,1,0:T(8,128)(2,1)}), bf16[32,128,128]{2,1,0:T(8,128)(2,1)}) %all-gather.6.cloned.1.call-update) | async-done | bytes 1048592 | tf_op jit(solution)/shard_map/all_gather | solution.py:432
  68.1 49.3 %all-gather.4.cloned.1.call-done.points_ref = bf16[1024,1024]{1,0:T(8,128)(2,1)} async-done(((bf16[64,1024]{1,0:T(8,128)(2,1)}), bf16[1024,1024]{1,0:T(8,128)(2,1)}) %all-gather.4.cloned.1.call-update) | async-done | bytes 2097168 | tf_op jit(solution)/shard_map/all_gather | solution.py:424
  117.4 4.3 %design.1 = (f32[128,1024]{1,0:T(8,128)}, s16[2,528,128]{2,1,0:T(8,128)(2,1)}) custom-call(bf16[16,2,128,128]{3,2,1,0:T(8,128)(2,1)} %bitcast.24, f32[128,128]{1,0:T(8,128)} %fusion.7.meta_ref, bf16[1024,1024]{1,0:T(8,128)(2,1)} %all-gather.4.cloned.1.call-done.points_ref), custom_call_target="tpu_custom_call" | custom-call | tf_op jit(solution)/shard_map/design/pallas_call | solution.py:387
  121.8 99.9 %gram.1 = f32[1024,1024]{1,0:T(8,128)} custom-call(s16[2,528,128]{2,1,0:T(8,128)(2,1)} %get-tuple-element.5.enc_ref), custom_call_target="tpu_custom_call" | custom-call | tf_op jit(solution)/shard_map/gram/pallas_call | solution.py:325
  221.7 4.8 %copy.33 = f32[1024,1024]{1,0:T(8,128)} copy(f32[1024,1024]{1,0:T(8,128)} %gram.1) | data formatting | bytes 8388608
  (18 shorter events, 1.4 us)
Async XLA Ops:
  7.2 2.5 %copy-start = (bf16[512,64]{0,1:T(8,128)(2,1)S(1)}, bf16[512,64]{0,1:T(8,128)(2,1)}, u32[]{:S(2)}) copy-start(bf16[512,64]{0,1:T(8,128)(2,1)} %param.6) | copy-start | bytes 196612
  13.8 12.7 %all-to-all-start = ((bf16[16,48,128]{2,1,0:T(8,128)(2,1)}), bf16[16,48,128]{2,1,0:T(8,128)(2,1)S(1)}, u32[]{:S(2)}, u32[]{:S(2)}) async-start(bf16[16,48,128]{2,1,0:T(8,128)(2,1)} %pad_maximum_fusion), calls=%async_computation | async-start | bytes 393216 | tf_op jit(solution)/shard_map/all_to_all | solution.py:426
  20.7 47.4 %all-gather.6.cloned.1.call-start = ((), (), s32[]{:S(2)}) async-start(), calls=%async_computation.2 | async-start | bytes 1114112 | tf_op jit(solution)/shard_map/all_gather | solution.py:432
  28.0 89.4 %all-gather.4.cloned.1.call-start = ((), (), s32[]{:S(2)}) async-start(), calls=%async_computation.1 | async-start | bytes 2228224 | tf_op jit(solution)/shard_map/all_gather | solution.py:424
Sparse Core Ops, SparseCore 0:
  28.1 39.9 all-gather.5
  70.5 46.8 all-gather.3

commit v2 on v1

v2 whole, which is shorter than its diff:
```python
import jax
import jax.numpy as jnp
from jax import lax
from jax.experimental import pallas as pl
from jax.experimental.pallas import tpu as pltpu
from jax.sharding import PartitionSpec as P

damping = 0.5
MESH = pl.DeviceIdType.MESH
f32, bf16, i16 = jnp.float32, jnp.bfloat16, jnp.int16
HALF = 528
CUT = 256
VMEM = pltpu.VMEM


def split_bf16(value):
    high = value.astype(bf16)
    return high, (value - high.astype(f32)).astype(bf16)


def where_am_i():
    r = lax.axis_index("rows")
    p = lax.axis_index("pts")
    return r // 4, r % 4, p // 2, p % 2


def plane_id(x, y, dx, dy):
    return ((x + dx + 4) % 4) * 4 + (y + dy + 4) % 4


def gather_keys():
    keys = []
    for half in (0, 1):
        for i in (0, 1, -1, 2):
            for j in (0, 1, -1, 2):
                if (i, j) == (0, 0):
                    continue
                two = j == 2 or (j == 0 and i == 2)
                keys += [(half, i, j, q) for q in ((0, 1) if two else (None,))]
    return {key: n for n, key in enumerate(keys)}


KEYS = gather_keys()


class TorusGather:
    def __init__(self, x, y, view, send_sems, recv_sems):
        self.x, self.y, self.view = x, y, view
        self.send_sems, self.recv_sems = send_sems, recv_sems
        self.sends = 0

    def offset(self, half, a, b):
        return (a, b) if half == 0 else (b, a)

    def block(self, half, i, j):
        return plane_id(self.x, self.y, *self.offset(half, i, j))

    def copy(self, half, i, j, q, to, key):
        target = plane_id(self.x, self.y, *self.offset(half, *to))
        block = self.block(half, i, j)
        pltpu.make_async_remote_copy(
            src_ref=self.view(block, half, q),
            dst_ref=self.view(block, half, q),
            send_sem=self.send_sems.at[self.sends],
            recv_sem=self.recv_sems.at[KEYS[key]],
            device_id={"rows": target},
            device_id_type=MESH,
        ).start()
        self.sends += 1

    def wait(self, half, i, j, q):
        ref = self.view(self.block(half, i, j), half, q)
        pltpu.make_async_copy(ref, ref, self.recv_sems.at[KEYS[(half, i, j, q)]]).wait()

    def start(self):
        for half in (0, 1):
            for d in (1, -1):
                self.copy(half, 0, 0, None, (d, 0), (half, -d, 0, None))
        for half in (0, 1):
            for d in (1, -1):
                self.copy(half, 0, 0, None, (0, d), (half, 0, -d, None))

    def first(self):
        for half in (0, 1):
            for d in (1, -1):
                q = 0 if d == 1 else 1
                self.wait(half, -d, 0, None)
                self.copy(half, -d, 0, q, (d, 0), (half, 2, 0, q))
                for e in (1, -1):
                    self.copy(half, -d, 0, None, (0, e), (half, -d, -e, None))

    def across(self, i):
        for half in (0, 1):
            for d in (1, -1):
                q = 0 if d == 1 else 1
                self.wait(half, i, -d, None)
                self.copy(half, i, -d, q, (0, d), (half, i, 2, q))

    def far(self):
        for half in (0, 1):
            for q in (0, 1):
                self.wait(half, 2, 0, q)
            for e in (1, -1):
                self.copy(half, 2, 0, None, (0, e), (half, 2, -e, None))

    def last(self, i):
        for half in (0, 1):
            for q in (0, 1):
                self.wait(half, i, 2, q)

    def drain(self):
        n = 0
        for whole in self.order():
            ref = self.view(0, 0, whole)
            pltpu.make_async_copy(ref, ref, self.send_sems.at[n]).wait()
            n += 1

    def order(self):
        sizes = [None] * 8
        for half in (0, 1):
            for d in (1, -1):
                sizes += [0 if d == 1 else 1, None, None]
        sizes += [0, 1] * 2
        sizes += [None] * 4
        sizes += [0, 1] * 2
        sizes += [0, 1] * 2
        sizes += [0, 1] * 2
        return sizes


ORDER = [(0, 0), (1, 0), (-1, 0), (0, 1), (0, -1), (2, 0), (1, 1), (1, -1), (-1, 1), (-1, -1),
         (0, 2), (2, 1), (2, -1), (1, 2), (-1, 2), (2, 2)]
FIRST_SLOT = 2
SLOTS = 50


def signed(value):
    return value - (1 << 32) if value >= 1 << 31 else value


FIRST_STEPS = signed(sum((a % 4) << (2 * n) for n, (a, b) in enumerate(ORDER)))
SECOND_STEPS = signed(sum((b % 4) << (2 * n) for n, (a, b) in enumerate(ORDER)))
PLANE = [(dx, dy) for dx in range(4) for dy in range(4) if (dx, dy) != (0, 0)]


def block_of(x, y, half, n):
    a = (jnp.int32(FIRST_STEPS) >> (2 * n)) & 3
    b = (jnp.int32(SECOND_STEPS) >> (2 * n)) & 3
    dx = jnp.where(half == 0, a, b)
    dy = jnp.where(half == 0, b, a)
    return ((x + dx) % 4) * 4 + (y + dy) % 4


def hop_slots(hops):
    return (7 * hops + 3) // 4


def column_scale(tile, factor):
    parts = tile.astype(jnp.int32).astype(f32)
    return jnp.exp2(parts[:8]) * (parts[8:] * (factor / 32767.0))


def as_i16(value):
    return jnp.clip(jnp.round(value), -32767.0, 32767.0).astype(jnp.int32).astype(i16)


def iota(shape, axis):
    return lax.broadcasted_iota(jnp.int32, shape, axis)


def one_hot(test):
    return jnp.where(test, 1.0, 0.0).astype(bf16)


def dot(a, b, ca=1, cb=0):
    return lax.dot_general(a, b, (((ca,), (cb,)), ((), ())), preferred_element_type=f32)


def fill_outbox(env_ref, index_ref, count_ref, weight_ref, dest_ref, outbox):
    row = dest_ref[...]
    live = row >= 0
    dest = row >> 7
    owner = jnp.where(dest == iota((256, 128), 1), 1.0, 0.0)
    earlier = dot(one_hot(iota((256, 256), 0) > iota((256, 256), 1)), owner.astype(bf16))
    rank = jnp.sum(earlier * owner, axis=1, keepdims=True)
    place = jnp.where(live, dest.astype(f32) * 16.0 + rank, 999.0)
    move = one_hot(place == iota((256, 256), 1).astype(f32))
    env = env_ref[...]
    sides = [dot(env, one_hot(iota((64, 128), 0) + 64 * k == iota((64, 128), 1))).astype(bf16) for k in (0, 1)]
    index = index_ref[...]
    envs = iota((256, 512), 1)
    picked = [
        (dot(one_hot(index[:, 2 * k : 2 * k + 1] == envs), sides[0])
         + dot(one_hot(index[:, 2 * k + 1 : 2 * k + 2] == envs), sides[1])).astype(bf16)
        for k in (0, 1)
    ]
    weight = jnp.where(iota((256, 4), 1) < count_ref[...], weight_ref[...], 0.0)
    lane = iota((256, 128), 1)
    within = jnp.where(live, (row & 127) + 1, 0).astype(f32)
    meta = jnp.where(lane == 12, within, 0.0)
    rest = weight
    for k in range(3):
        part = rest.astype(bf16).astype(f32)
        rest = rest - part
        for j in range(4):
            meta = jnp.where(lane == 4 * k + j, part[:, j : j + 1], meta)
    moved = dot(move, jnp.concatenate(picked + [meta.astype(bf16)], axis=1), 0, 0).astype(bf16)
    for d in range(16):
        for k in range(3):
            outbox[d, 16 * k : 16 * k + 16, :] = moved[16 * d : 16 * d + 16, 128 * k : 128 * k + 128]


def whole_kernel(env_ref, desc_ref, index_ref, count_ref, weight_ref, dest_ref, design_ref, out_ref,
                 points, outbox, inbox, feats, meta, lhs, buf, hp, lp, hrt, lrt,
                 psend, precv, osend, orecv, own_sem, fsend, frecv, frecv2, sends, recvs, zsends, zrecvs):
    x, y, z, c = where_am_i()
    r = x * 4 + y
    p = z * 2 + c
    z0, c0 = r // 2, r % 2
    dz = (z - z0 + 8) % 8
    root_chip = dz == 0
    root = jnp.logical_and(root_chip, c == c0)
    up = {"pts": ((z + 1) % 8) * 2}
    down = {"pts": ((z + 7) % 8) * 2 + 1}
    other = {"pts": z * 2 + 1 - c}
    along = {1: {"pts": ((z + 1) % 8) * 2 + c}, -1: {"pts": ((z + 7) % 8) * 2 + c}}
    barrier = pltpu.get_barrier_semaphore()
    for dx, dy in PLANE:
        pl.semaphore_signal(barrier, inc=1, device_id={"rows": plane_id(x, y, dx, dy)}, device_id_type=MESH)
    for dc in (0, 1):
        for target in ((z + 1) % 8, (z + 7) % 8):
            pl.semaphore_signal(barrier, inc=1, device_id={"pts": target * 2 + dc}, device_id_type=MESH)
    pl.semaphore_signal(barrier, inc=1, device_id=other, device_id_type=MESH)

    own = dot(one_hot(iota((64, 64), 0) == iota((64, 64), 1)), desc_ref[...], 1, 1).astype(bf16)
    points[r, 0] = own[:32]
    points[r, 1] = own[32:]
    fill_outbox(env_ref, index_ref, count_ref, weight_ref, dest_ref, outbox)
    pl.semaphore_wait(barrier, 20)

    def post(k, dx, dy):
        target = plane_id(x, y, dx, dy)
        return pltpu.make_async_remote_copy(
            src_ref=outbox.at[target], dst_ref=inbox.at[r], send_sem=osend.at[k], recv_sem=orecv.at[k],
            device_id={"rows": target}, device_id_type=MESH,
        )

    for k, (dx, dy) in enumerate(PLANE):
        post(k, dx, dy).start()
    own_copy = pltpu.make_async_copy(outbox.at[r], inbox.at[r], own_sem)
    own_copy.start()

    def points_view(block, half, q):
        return points.at[block, half] if q is None else points.at[block, half, pl.ds(16 * q, 16)]

    spread = TorusGather(x, y, points_view, psend, precv)
    spread.start()

    rows = r * 1024 + iota((128, 1024), 0)
    cols = p * 1024 + iota((128, 1024), 1)

    @pl.loop(0, 8)
    def _(m):
        out_ref[pl.ds(pl.multiple_of(m * 128, 128), 128), :] = jnp.where(rows + m * 128 == cols, damping, 0.0)

    spread.first()
    own_copy.wait()
    for k, (dx, dy) in enumerate(PLANE):
        ref = inbox.at[plane_id(x, y, -dx, -dy)]
        pltpu.make_async_copy(ref, ref, orecv.at[k]).wait()
    arrived = [jnp.concatenate([inbox[g, 16 * k : 16 * k + 16, :] for g in range(16)], axis=0) for k in range(3)]
    spots = arrived[2][:, 12:13].astype(f32)
    put = one_hot(spots == (iota((256, 128), 1) + 1).astype(f32))
    placed = dot(put, jnp.concatenate(arrived, axis=1), 0, 0)
    feats[p, 0] = placed[:, :128].astype(bf16)
    feats[p, 1] = placed[:, 128:256].astype(bf16)
    meta[...] = placed[:, 256:]

    def feat_copy(offset, pair, target, n, recv):
        ref = feats.at[((z + offset + 8) % 8) * 2 + c]
        if pair is not None:
            ref = ref.at[pair]
        return pltpu.make_async_remote_copy(
            src_ref=ref, dst_ref=ref, send_sem=fsend.at[n], recv_sem=recv, device_id=target, device_id_type=MESH
        )

    def feat_wait(owner, sem, pair=None):
        ref = feats.at[owner]
        if pair is not None:
            ref = ref.at[pair]
        pltpu.make_async_copy(ref, ref, sem).wait()

    feat_copy(0, None, along[1], 0, frecv.at[0]).start()
    feat_copy(0, None, along[-1], 1, frecv.at[4]).start()
    feat_copy(0, None, other, 2, frecv2.at[0]).start()

    def feat_step(k):
        for d, base in ((1, 0), (-1, 4)):
            pair = (0 if d == 1 else 1) if k == 3 else None
            n = 3 + 4 * (k - 1) + (0 if d == 1 else 2)
            feat_wait(((z - d * k + 8) % 8) * 2 + c, frecv.at[base + k - 1])
            feat_copy(-d * k, pair, along[d], n, frecv.at[base + k]).start()
            feat_copy(-d * k, None, other, n + 1, frecv2.at[(8 - d * k) % 8]).start()

    spread.across(0)
    feat_step(1)
    spread.far()
    feat_step(2)
    spread.across(1)
    feat_step(3)
    spread.across(-1)
    for d, base, pair in ((1, 0, 0), (-1, 4, 1)):
        feat_wait(((z + 4) % 8) * 2 + c, frecv.at[base + 3], pair)
    feat_copy(4, None, other, 15, frecv2.at[4]).start()
    for k in range(8):
        feat_wait(((z + k) % 8) * 2 + 1 - c, frecv2.at[k])
    spread.across(2)
    lane = iota((128, 128), 1)
    for k in range(8):
        for pair in (0, 1):
            a = feats[2 * k, pair].astype(f32)
            b = feats[2 * k + 1, pair].astype(f32)
            even = jnp.where(lane < 64, a, pltpu.roll(b, 64, 1))
            odd = jnp.where(lane < 64, pltpu.roll(a, 64, 1), b)
            lhs[pl.ds(pair * 256, 128), pl.ds(k * 128, 128)] = even.astype(bf16)
            lhs[pl.ds(pair * 256 + 128, 128), pl.ds(k * 128, 128)] = odd.astype(bf16)
    for i in (0, 1, -1, 2):
        spread.last(i)

    coeffs = meta[...]
    weights = [coeffs[:, j : j + 1] + coeffs[:, j + 4 : j + 5] + coeffs[:, j + 8 : j + 9] for j in range(4)]
    tops, bottoms = [], []
    for t in range(4):
        span = pl.ds(t * 256, 256)
        products = dot(lhs[...], points[:, :, :, span].reshape(1024, 256))
        scaled = products * (1.0 / 32.0)
        squared = scaled * scaled
        values = 0.25 * squared * squared
        line = jnp.zeros((128, 256), f32)
        for j in range(4):
            line = line + weights[j] * values[j * 128 : (j + 1) * 128]
        design_ref[:, span] = line
        largest = jnp.maximum(jnp.max(jnp.abs(line), axis=0, keepdims=True), 1e-30)
        exponent = jnp.floor(jnp.log2(largest)) - 14.0
        mantissa = jnp.minimum(jnp.ceil(largest * jnp.exp2(-exponent)), 32767.0)
        coded = line * (32767.0 / (mantissa * jnp.exp2(exponent)))
        for u in range(2):
            j = 2 * t + u
            part = as_i16(coded[:, 128 * u : 128 * u + 128])
            for half in (0, 1):
                buf[0, r, half, pl.ds(64 * j, 64), :] = part[64 * half : 64 * half + 64]
            tops.append(exponent[:, 128 * u : 128 * u + 128])
            bottoms.append(mantissa[:, 128 * u : 128 * u + 128])
    tile = as_i16(jnp.concatenate(tops + bottoms, axis=0))
    buf[0, r, 0, pl.ds(512, 16), :] = tile
    buf[0, r, 1, pl.ds(512, 16), :] = tile

    def panel_view(block, half, q):
        ref = buf.at[0, block, half]
        if q is None:
            return ref
        return ref.at[pl.ds(0, CUT)] if q == 0 else ref.at[pl.ds(CUT, HALF - CUT)]

    gather = TorusGather(x, y, panel_view, sends, recvs)
    gather.start()

    def z_copy(block, half, target, n, k):
        return pltpu.make_async_remote_copy(
            src_ref=buf.at[jnp.where(root, 0, 1), block, half],
            dst_ref=buf.at[1, block, half],
            send_sem=zsends.at[n, k],
            recv_sem=zrecvs.at[n, half],
            device_id=target,
            device_id_type=MESH,
        )

    def z_wait(block, half, n):
        ref = buf.at[1, block, half]
        pltpu.make_async_copy(ref, ref, zrecvs.at[n, half]).wait()

    hops = jnp.where(c == 0, dz, (8 - dz) % 8)
    not_end = hops != 7

    def pass_on(n):
        @pl.when(root)
        def _():
            for half in (0, 1):
                block = block_of(x, y, half, n)
                z_copy(block, half, up if half == 0 else down, n, half).start()
                z_copy(block, half, other, n, half + 2).start()

        for half in (0, 1):
            @pl.when(jnp.logical_and(jnp.logical_not(root_chip), c == half))
            def _():
                block = block_of(x, y, half, n)
                z_wait(block, half, n)

                @pl.when(not_end)
                def _():
                    z_copy(block, half, up if half == 0 else down, n, 0).start()

                z_copy(block, half, other, n, 1).start()

    def drained(n):
        ref = buf.at[0, 0, 0]

        @pl.when(root)
        def _():
            for k in range(4):
                pltpu.make_async_copy(ref, ref, zsends.at[n, k]).wait()

        @pl.when(jnp.logical_not(root_chip))
        def _():
            @pl.when(not_end)
            def _():
                pltpu.make_async_copy(ref, ref, zsends.at[n, 0]).wait()

            pltpu.make_async_copy(ref, ref, zsends.at[n, 1]).wait()

    from_root = jnp.where(root, 0, 1)

    def decode(half, u):
        for v in (0, 1):
            blocks = [block_of(x, y, half, 4 * u + 2 * v + k) for k in (0, 1)]

            @pl.when(jnp.logical_and(jnp.logical_not(root), jnp.logical_or(root_chip, c != half)))
            def _():
                for k in (0, 1):
                    z_wait(blocks[k], half, 4 * u + 2 * v + k)

            scale_p = [column_scale(buf[0, b, half, pl.ds(512, 16), :], 2.0 ** -11) for b in blocks]
            scale_r = [column_scale(buf[from_root, b, half, pl.ds(512, 16), :], 1.0) for b in blocks]
            for j in range(8):
                span = slice(128 * j, 128 * j + 128)
                piece = pl.ds(64 * j, 64)
                both_p = jnp.concatenate([
                    buf[0, b, half, piece, :].astype(jnp.int32).astype(f32) * scale[j : j + 1, :]
                    for b, scale in zip(blocks, scale_p)
                ], axis=0)
                spot = pl.ds(v * 128, 128)
                hp[half, spot, span], lp[half, spot, span] = split_bf16(both_p)
                both_r = jnp.concatenate([
                    buf[from_root, b, half, piece, :].astype(jnp.int32).astype(f32) * scale[j : j + 1, :]
                    for b, scale in zip(blocks, scale_r)
                ], axis=0)
                hrt[half, span, spot], lrt[half, span, spot] = split_bf16(both_r.T)

    def multiply(half, t):
        span = pl.ds(pl.multiple_of(t * 256, 256), 256)
        high = hrt[half]
        left = jnp.concatenate([high, high, lrt[half]], axis=1)
        right_high = hp[half, :, span]
        right = jnp.concatenate([right_high, lp[half, :, span], right_high], axis=0)
        out_ref[:, span] += dot(left, right)

    events = {
        2: gather.first, 5: lambda: gather.across(0), 6: gather.far, 8: lambda: gather.across(1),
        10: lambda: gather.across(-1), 12: lambda: gather.last(0), 13: lambda: gather.across(2),
        15: lambda: gather.last(1), 16: lambda: gather.last(-1), 17: lambda: gather.last(2),
    }

    @pl.loop(FIRST_SLOT, FIRST_SLOT + 16 + 13 + 8)
    def _(s):
        for slot, event in events.items():
            pl.when(s == slot)(event)
        n = s - FIRST_SLOT - hop_slots(hops)

        @pl.when(jnp.logical_and(n >= 0, n < 16))
        def _():
            pass_on(n)

        @pl.loop(0, 2)
        def _(half):
            steps = hop_slots(jnp.where(half == 0, dz, (8 - dz) % 8))
            late = jnp.where(jnp.logical_or(root, jnp.logical_and(half == c, jnp.logical_not(root_chip))), 0, 1)
            m = s - FIRST_SLOT - steps - late - 3

            @pl.when(jnp.logical_and(m >= 0, m < 16))
            def _():
                @pl.when(m % 4 == 0)
                def _():
                    decode(half, m // 4)

                multiply(half, m % 4)

    spread.drain()
    gather.drain()
    for k, (dx, dy) in enumerate(PLANE):
        post(k, dx, dy).wait_send()
    for n in range(3):
        feat_wait(0, fsend.at[n])
    for k in (1, 2, 3):
        for d in (1, -1):
            n = 3 + 4 * (k - 1) + (0 if d == 1 else 2)
            feat_wait(0, fsend.at[n], 0 if k == 3 else None)
            feat_wait(0, fsend.at[n + 1])
    feat_wait(0, fsend.at[15])

    @pl.loop(0, 16)
    def _(n):
        drained(n)


def on_device(env_desc, point_desc, pool_index, pool_count, pool_weight, row_dest):
    sem = pltpu.SemaphoreType.DMA
    return pl.pallas_call(
        whole_kernel,
        out_shape=(jax.ShapeDtypeStruct((128, 1024), f32), jax.ShapeDtypeStruct((1024, 1024), f32)),
        in_specs=[pl.BlockSpec(memory_space=VMEM)] * 6,
        out_specs=(pl.BlockSpec(memory_space=VMEM), pl.BlockSpec(memory_space=VMEM)),
        scratch_shapes=[
            VMEM((16, 2, 32, 1024), bf16),
            VMEM((16, 48, 128), bf16),
            VMEM((16, 48, 128), bf16),
            VMEM((16, 2, 128, 128), bf16),
            VMEM((128, 128), f32),
            VMEM((512, 1024), bf16),
            VMEM((2, 16, 2, HALF, 128), i16),
            VMEM((2, 256, 1024), bf16),
            VMEM((2, 256, 1024), bf16),
            VMEM((2, 1024, 256), bf16),
            VMEM((2, 1024, 256), bf16),
            sem((40,)), sem((40,)), sem((15,)), sem((15,)), sem(()), sem((16,)), sem((8,)), sem((8,)),
            sem((40,)), sem((40,)), sem((16, 4)), sem((16, 2)),
        ],
        compiler_params=pltpu.CompilerParams(collective_id=1, has_side_effects=True, vmem_limit_bytes=56 << 20),
        name="whole",
    )(env_desc, point_desc, pool_index, pool_count.reshape(256, 1), pool_weight, row_dest.reshape(256, 1))


def solution(mesh):
    in_specs = (
        P("rows", "pts"),
        P("pts", "rows"),
        P("rows", None),
        P("rows"),
        P("rows", None),
        P("rows"),
    )
    out_specs = (P("rows", "pts"), P("rows", "pts"))
    return jax.shard_map(
        on_device, mesh=mesh, in_specs=in_specs, out_specs=out_specs, check_vma=False
    )
```

time: 234 us -> 131 us (0.56)
  waiting for transfers between devices: 94.2 us -> 0 us
  between operations: 14.1 us -> 0.64 us
  Pallas kernels: 104 us -> 113 us
  local copies, waits for them, and re-layouts: 6.94 us -> 15.9 us
  starting transfers between devices: 7 us -> 0 us
  other arithmetic: 3.64 us -> 0 us
  matrix products: 3.09 us -> 0 us
    all_gather x2 -> x0, waiting for transfers between devices: 87.8 us -> none  [the longest x1 49.3 us: on_device(): points = lax.all_gather(point_desc.T, 'rows', axis=0, tiled=True)]
    pallas_call x2 -> x1, Pallas kernels: 104 us -> 113 us  [on_device(): pl.pallas_call(whole_kernel, out_shape=(jax.ShapeDtypeStruct((128, 1024),...]
    unnamed x3 -> x6, local copies, waits for them, and re-layouts: 4.8 us -> 13 us
    all_to_all x1 -> x0, starting transfers between devices: 6.92 us -> none  [on_device(): lax.all_to_all(outbox, 'rows', split_axis=0, concat_axis=0, tiled=True)]
    all_to_all x1 -> x0, waiting for transfers between devices: 5.74 us -> none  [on_device(): lax.all_to_all(outbox, 'rows', split_axis=0, concat_axis=0, tiled=True)]
    dot_general x9 -> x0, matrix products: 3.09 us -> none  [the longest x3 1.49 us: on_device(): lax.dot_general(put, part, (((0,), (0,)), ((), ())), preferred_element_ty...]
    reshape x0 -> x2, local copies, waits for them, and re-layouts: none -> 2.95 us  [the longest x1 1.47 us: on_device(): pool_count.reshape(256, 1)]
  transfers between devices with their start and end apart: 3 -> 0, of which waited for: 3 -> 0; matrix products, arithmetic and copies ran while one was open for 0% -> 0% of each run, Pallas kernels for 0% -> 0%
where the time goes in v2:
time: 131 us; the launch traced here: 130 us
  Pallas kernels  113 us (86%)
  local copies, waits for them, and re-layouts  15.9 us (12%)
    pallas_call x1, Pallas kernels, on_device(): pl.pallas_call(whole_kernel, out_shape=(jax.ShapeDtypeStruct((128, 1024),...  113 us
    unnamed x6, local copies, waits for them, and re-layouts  13 us

profile of v2, /device:TPU:35, one launch (start us, length us, event | category | flops | bytes accessed | tf_op | source)
XLA Modules:
  0.0 129.8 jit_solution(8128613793998473884)
XLA Ops:
  0.6 1.6 %copy.12.env_ref = bf16[512,64]{1,0:T(8,128)(2,1)} copy(bf16[512,64]{0,1:T(8,128)(2,1)} %param.6) | data formatting | bytes 131072 | tf_op args[0]
  2.2 1.5 %copy.14.index_ref = s32[256,4]{1,0:T(8,128)} copy(s32[256,4]{0,1:T(4,128)} %param.8) | data formatting | bytes 8192 | tf_op args[2]
  3.7 1.5 %copy.15.count_ref = s32[256,1]{1,0:T(8,128)} copy(s32[256,1]{0,1:T(1,128)} %bitcast.2) | data formatting | bytes 2048 | tf_op jit(solution)/shard_map/reshape | solution.py:528
  5.2 1.5 %copy.16.weight_ref = f32[256,4]{1,0:T(8,128)} copy(f32[256,4]{0,1:T(4,128)} %param.10) | data formatting | bytes 8192 | tf_op args[4]
  6.7 1.5 %copy.17.dest_ref = s32[256,1]{1,0:T(8,128)} copy(s32[256,1]{0,1:T(1,128)} %bitcast.3) | data formatting | bytes 2048 | tf_op jit(solution)/shard_map/reshape | solution.py:528
  8.1 1.7 %copy.13.desc_ref = bf16[1024,64]{1,0:T(8,128)(2,1)} copy(bf16[1024,64]{0,1:T(8,128)(2,1)} %param.7) | data formatting | bytes 262144 | tf_op args[1]
  9.9 113.2 %whole.1 = (f32[128,1024]{1,0:T(8,128)}, f32[1024,1024]{1,0:T(8,128)}) custom-call(bf16[512,64]{1,0:T(8,128)(2,1)} %copy.12.env_ref, bf16[1024,64]{1,0:T(8,128)(2,1)} %copy.13.desc_ref, s32[256,4]{1,0:T(8,128)} %copy.14.index_ref, s32[256,1]{1,0:T(8,128)} %copy.15.count_ref, f32[256,4]{1,0:T(8,128)} %copy.16.weight_ref, s32[256,1]{1,0:T(8,128)} %copy.17.dest_ref), custom_call_target="tpu_custom_call" | custom-call | tf_op jit(solution)/shard_map/whole/pallas_call | solution.py:506
  123.1 1.9 %copy.20 = f32[128,1024]{1,0:T(8,128)} copy(f32[128,1024]{1,0:T(8,128)} %get-tuple-element.4) | data formatting | bytes 1048576
  125.0 4.8 %copy.21 = f32[1024,1024]{1,0:T(8,128)} copy(f32[1024,1024]{1,0:T(8,128)} %get-tuple-element.5) | data formatting | bytes 8388608

commit v3 on v2

--- a/solution.py
+++ b/solution.py
@@ -180,31 +180,26 @@
     row = dest_ref[...]
     live = row >= 0
     dest = row >> 7
-    owner = jnp.where(dest == iota((256, 128), 1), 1.0, 0.0)
-    earlier = dot(one_hot(iota((256, 256), 0) > iota((256, 256), 1)), owner.astype(bf16))
-    rank = jnp.sum(earlier * owner, axis=1, keepdims=True)
+    owner = jnp.where(dest == iota((16, 256), 0), 1.0, 0.0)
+    earlier = dot(owner.astype(bf16), one_hot(iota((256, 256), 0) < iota((256, 256), 1)))
+    rank = jnp.sum(earlier * owner, axis=0, keepdims=True)
     place = jnp.where(live, dest.astype(f32) * 16.0 + rank, 999.0)
-    move = one_hot(place == iota((256, 256), 1).astype(f32))
+    move = one_hot(place == iota((256, 256), 0).astype(f32))
     env = env_ref[...]
-    sides = [dot(env, one_hot(iota((64, 128), 0) + 64 * k == iota((64, 128), 1))).astype(bf16) for k in (0, 1)]
     index = index_ref[...]
-    envs = iota((256, 512), 1)
-    picked = [
-        (dot(one_hot(index[:, 2 * k : 2 * k + 1] == envs), sides[0])
-         + dot(one_hot(index[:, 2 * k + 1 : 2 * k + 2] == envs), sides[1])).astype(bf16)
-        for k in (0, 1)
-    ]
-    weight = jnp.where(iota((256, 4), 1) < count_ref[...], weight_ref[...], 0.0)
-    lane = iota((256, 128), 1)
-    within = jnp.where(live, (row & 127) + 1, 0).astype(f32)
-    meta = jnp.where(lane == 12, within, 0.0)
-    rest = weight
-    for k in range(3):
+    envs = iota((512, 256), 0)
+    picked = [dot(env, one_hot(index[j : j + 1] == envs)).astype(bf16) for j in range(4)]
+    rest = jnp.where(iota((4, 256), 0) < count_ref[...], weight_ref[...], 0.0)
+    meta = []
+    for _ in range(3):
         part = rest.astype(bf16).astype(f32)
         rest = rest - part
-        for j in range(4):
-            meta = jnp.where(lane == 4 * k + j, part[:, j : j + 1], meta)
-    moved = dot(move, jnp.concatenate(picked + [meta.astype(bf16)], axis=1), 0, 0).astype(bf16)
+        meta.append(part)
+    within = jnp.where(live, (row & 127) + 1, 0).astype(f32)
+    meta.append(jnp.where(iota((4, 256), 0) == 0, within, 0.0))
+    meta.append(jnp.zeros((112, 256), f32))
+    everything = jnp.concatenate(picked + [jnp.concatenate(meta, axis=0).astype(bf16)], axis=0)
+    moved = dot(move, everything, 1, 1).astype(bf16)
     for d in range(16):
         for k in range(3):
             outbox[d, 16 * k : 16 * k + 16, :] = moved[16 * d : 16 * d + 16, 128 * k : 128 * k + 128]
@@ -224,19 +219,20 @@
     down = {"pts": ((z + 7) % 8) * 2 + 1}
     other = {"pts": z * 2 + 1 - c}
     along = {1: {"pts": ((z + 1) % 8) * 2 + c}, -1: {"pts": ((z + 7) % 8) * 2 + c}}
+    beyond = {1: {"pts": ((z + 2) % 8) * 2 + c}, -1: {"pts": ((z + 6) % 8) * 2 + c}}
     barrier = pltpu.get_barrier_semaphore()
     for dx, dy in PLANE:
         pl.semaphore_signal(barrier, inc=1, device_id={"rows": plane_id(x, y, dx, dy)}, device_id_type=MESH)
     for dc in (0, 1):
         for target in ((z + 1) % 8, (z + 7) % 8):
             pl.semaphore_signal(barrier, inc=1, device_id={"pts": target * 2 + dc}, device_id_type=MESH)
-    pl.semaphore_signal(barrier, inc=1, device_id=other, device_id_type=MESH)
-
-    own = dot(one_hot(iota((64, 64), 0) == iota((64, 64), 1)), desc_ref[...], 1, 1).astype(bf16)
-    points[r, 0] = own[:32]
-    points[r, 1] = own[32:]
+    for target in (other, beyond[1], beyond[-1]):
+        pl.semaphore_signal(barrier, inc=1, device_id=target, device_id_type=MESH)
+
+    points[r, 0] = desc_ref[:32]
+    points[r, 1] = desc_ref[32:]
     fill_outbox(env_ref, index_ref, count_ref, weight_ref, dest_ref, outbox)
-    pl.semaphore_wait(barrier, 20)
+    pl.semaphore_wait(barrier, 22)
 
     def post(k, dx, dy):
         target = plane_id(x, y, dx, dy)
@@ -290,24 +286,29 @@
             ref = ref.at[pair]
         pltpu.make_async_copy(ref, ref, sem).wait()
 
-    feat_copy(0, None, along[1], 0, frecv.at[0]).start()
-    feat_copy(0, None, along[-1], 1, frecv.at[4]).start()
-    feat_copy(0, None, other, 2, frecv2.at[0]).start()
+    for n, (target, recv) in enumerate((
+        (along[1], frecv.at[0]), (along[-1], frecv.at[4]), (beyond[1], frecv.at[1]), (beyond[-1], frecv.at[5]),
+        (other, frecv2.at[0]),
+    )):
+        feat_copy(0, None, target, n, recv).start()
 
     def feat_step(k):
         for d, base in ((1, 0), (-1, 4)):
-            pair = (0 if d == 1 else 1) if k == 3 else None
-            n = 3 + 4 * (k - 1) + (0 if d == 1 else 2)
+            n = 4 * k + 1 + (0 if d == 1 else 2)
             feat_wait(((z - d * k + 8) % 8) * 2 + c, frecv.at[base + k - 1])
-            feat_copy(-d * k, pair, along[d], n, frecv.at[base + k]).start()
+            if k < 3:
+                pair = None if k == 1 else base // 4
+                feat_copy(-d * k, pair, beyond[d], n, frecv.at[base + k + 1]).start()
+            else:
+                n = 12 if d == 1 else 13
             feat_copy(-d * k, None, other, n + 1, frecv2.at[(8 - d * k) % 8]).start()
 
+    feat_step(1)
     spread.across(0)
-    feat_step(1)
+    feat_step(2)
     spread.far()
-    feat_step(2)
+    feat_step(3)
     spread.across(1)
-    feat_step(3)
     spread.across(-1)
     for d, base, pair in ((1, 0, 0), (-1, 4, 1)):
         feat_wait(((z + 4) % 8) * 2 + c, frecv.at[base + 3], pair)
@@ -487,14 +488,8 @@
     gather.drain()
     for k, (dx, dy) in enumerate(PLANE):
         post(k, dx, dy).wait_send()
-    for n in range(3):
-        feat_wait(0, fsend.at[n])
-    for k in (1, 2, 3):
-        for d in (1, -1):
-            n = 3 + 4 * (k - 1) + (0 if d == 1 else 2)
-            feat_wait(0, fsend.at[n], 0 if k == 3 else None)
-            feat_wait(0, fsend.at[n + 1])
-    feat_wait(0, fsend.at[15])
+    for n in range(16):
+        feat_wait(0, fsend.at[n], 0 if n in (9, 11) else None)
 
     @pl.loop(0, 16)
     def _(n):
@@ -505,7 +500,7 @@
     sem = pltpu.SemaphoreType.DMA
     return pl.pallas_call(
         whole_kernel,
-        out_shape=(jax.ShapeDtypeStruct((128, 1024), f32), jax.ShapeDtypeStruct((1024, 1024), f32)),
+        out_shape=(pltpu.VMEM((128, 1024), f32), pltpu.VMEM((1024, 1024), f32)),
         in_specs=[pl.BlockSpec(memory_space=VMEM)] * 6,
         out_specs=(pl.BlockSpec(memory_space=VMEM), pl.BlockSpec(memory_space=VMEM)),
         scratch_shapes=[
@@ -525,7 +520,7 @@
         ],
         compiler_params=pltpu.CompilerParams(collective_id=1, has_side_effects=True, vmem_limit_bytes=56 << 20),
         name="whole",
-    )(env_desc, point_desc, pool_index, pool_count.reshape(256, 1), pool_weight, row_dest.reshape(256, 1))
+    )(env_desc.T, point_desc.T, pool_index.T, pool_count.reshape(1, 256), pool_weight.T, row_dest.reshape(1, 256))
 
 
 def solution(mesh):

time: 131 us -> 113 us (0.86)
  local copies, waits for them, and re-layouts: 15.9 us -> 2.81 us
  Pallas kernels: 113 us -> 109 us
    unnamed x6 -> x2, local copies, waits for them, and re-layouts: 13 us -> 2.81 us
    pallas_call x1, Pallas kernels: 113 us -> 109 us  [on_device(): pl.pallas_call(whole_kernel, out_shape=(pltpu.VMEM((128, 1024), f32), plt...]
    reshape x2 -> x0, local copies, waits for them, and re-layouts: 2.95 us -> none  [the longest x1 1.47 us: on_device(): pool_count.reshape(256, 1)]
where the time goes in v3:
time: 113 us
  Pallas kernels  109 us (96%)
  local copies, waits for them, and re-layouts  2.81 us (2%)
    pallas_call x1, Pallas kernels, on_device(): pl.pallas_call(whole_kernel, out_shape=(pltpu.VMEM((128, 1024), f32), plt...  109 us
    unnamed x2, local copies, waits for them, and re-layouts  2.81 us

profile of v3, /device:TPU:35, one launch (start us, length us, event | category | flops | bytes accessed | tf_op | source)
XLA Modules:
  0.0 112.5 jit_solution(10950238652302388594)
XLA Ops:
  0.6 109.1 %whole.1 = (f32[128,1024]{1,0:T(8,128)S(1)}, f32[1024,1024]{1,0:T(8,128)S(1)}) custom-call(bf16[64,512]{1,0:T(8,128)(2,1)} %bitcast.7, bf16[64,1024]{1,0:T(8,128)(2,1)} %bitcast.6, s32[4,256]{1,0:T(4,128)} %bitcast.8, s32[1,256]{1,0:T(1,128)} %bitcast.10, f32[4,256]{1,0:T(4,128)} %bitcast.9, s32[1,256]{1,0:T(1,128)} %bitcast.11), custom_call_target="tpu_custom_call" | custom-call | tf_op jit(solution)/shard_map/whole/pallas_call | solution.py:501
  109.7 0.8 copy.10
  110.5 2.0 %copy.11 = f32[1024,1024]{1,0:T(8,128)} copy(f32[1024,1024]{1,0:T(8,128)S(1)} %get-tuple-element.3) | data formatting | bytes 8388608

commit v4 on v3

--- a/solution.py
+++ b/solution.py
@@ -128,31 +128,7 @@
         return sizes
 
 
-ORDER = [(0, 0), (1, 0), (-1, 0), (0, 1), (0, -1), (2, 0), (1, 1), (1, -1), (-1, 1), (-1, -1),
-         (0, 2), (2, 1), (2, -1), (1, 2), (-1, 2), (2, 2)]
-FIRST_SLOT = 2
-SLOTS = 50
-
-
-def signed(value):
-    return value - (1 << 32) if value >= 1 << 31 else value
-
-
-FIRST_STEPS = signed(sum((a % 4) << (2 * n) for n, (a, b) in enumerate(ORDER)))
-SECOND_STEPS = signed(sum((b % 4) << (2 * n) for n, (a, b) in enumerate(ORDER)))
 PLANE = [(dx, dy) for dx in range(4) for dy in range(4) if (dx, dy) != (0, 0)]
-
-
-def block_of(x, y, half, n):
-    a = (jnp.int32(FIRST_STEPS) >> (2 * n)) & 3
-    b = (jnp.int32(SECOND_STEPS) >> (2 * n)) & 3
-    dx = jnp.where(half == 0, a, b)
-    dy = jnp.where(half == 0, b, a)
-    return ((x + dx) % 4) * 4 + (y + dy) % 4
-
-
-def hop_slots(hops):
-    return (7 * hops + 3) // 4
 
 
 def column_scale(tile, factor):
@@ -207,32 +183,36 @@
 
 def whole_kernel(env_ref, desc_ref, index_ref, count_ref, weight_ref, dest_ref, design_ref, out_ref,
                  points, outbox, inbox, feats, meta, lhs, buf, hp, lp, hrt, lrt,
-                 psend, precv, osend, orecv, own_sem, fsend, frecv, frecv2, sends, recvs, zsends, zrecvs):
+                 psend, precv, osend, orecv, own_sem, fsend, frecv, frecv2, sends, recvs, middle, rsend, rrecv, tsend, trecv, zsend, zrecv, zsend2, zrecv2):
     x, y, z, c = where_am_i()
     r = x * 4 + y
     p = z * 2 + c
-    z0, c0 = r // 2, r % 2
-    dz = (z - z0 + 8) % 8
-    root_chip = dz == 0
-    root = jnp.logical_and(root_chip, c == c0)
-    up = {"pts": ((z + 1) % 8) * 2}
-    down = {"pts": ((z + 7) % 8) * 2 + 1}
+    lift = (7 * p + 16 - r) % 16
+    drop = (7 * (p + r)) % 16
+    source = (7 * r + 16 - p) % 16
+    lifts, drops = lift != p, drop != r
     other = {"pts": z * 2 + 1 - c}
     along = {1: {"pts": ((z + 1) % 8) * 2 + c}, -1: {"pts": ((z + 7) % 8) * 2 + c}}
     beyond = {1: {"pts": ((z + 2) % 8) * 2 + c}, -1: {"pts": ((z + 6) % 8) * 2 + c}}
     barrier = pltpu.get_barrier_semaphore()
     for dx, dy in PLANE:
         pl.semaphore_signal(barrier, inc=1, device_id={"rows": plane_id(x, y, dx, dy)}, device_id_type=MESH)
-    for dc in (0, 1):
-        for target in ((z + 1) % 8, (z + 7) % 8):
-            pl.semaphore_signal(barrier, inc=1, device_id={"pts": target * 2 + dc}, device_id_type=MESH)
+    for d in (1, -1):
+        pl.semaphore_signal(barrier, inc=1, device_id=along[d], device_id_type=MESH)
+
+    for moves, targets in ((lifts, ({"pts": lift}, {"pts": drop})), (drops, ({"rows": drop}, {"rows": source}))):
+        @pl.when(moves)
+        def _():
+            for target in targets:
+                pl.semaphore_signal(barrier, inc=1, device_id=target, device_id_type=MESH)
+
     for target in (other, beyond[1], beyond[-1]):
         pl.semaphore_signal(barrier, inc=1, device_id=target, device_id_type=MESH)
 
     points[r, 0] = desc_ref[:32]
     points[r, 1] = desc_ref[32:]
     fill_outbox(env_ref, index_ref, count_ref, weight_ref, dest_ref, outbox)
-    pl.semaphore_wait(barrier, 22)
+    pl.semaphore_wait(barrier, 20 + jnp.where(lifts, 2, 0) + jnp.where(drops, 2, 0))
 
     def post(k, dx, dy):
         target = plane_id(x, y, dx, dy)
@@ -362,127 +342,118 @@
             return ref
         return ref.at[pl.ds(0, CUT)] if q == 0 else ref.at[pl.ds(CUT, HALF - CUT)]
 
+    def rise(half):
+        return pltpu.make_async_remote_copy(
+            src_ref=buf.at[0, r, half], dst_ref=middle.at[half], send_sem=rsend.at[half], recv_sem=rrecv.at[half],
+            device_id={"pts": lift}, device_id_type=MESH,
+        )
+
+    def turn(half):
+        return pltpu.make_async_remote_copy(
+            src_ref=middle.at[half], dst_ref=buf.at[1, p, half], send_sem=tsend.at[half], recv_sem=trecv.at[half],
+            device_id={"rows": drop}, device_id_type=MESH,
+        )
+
+    for half in (0, 1):
+        pl.when(lifts)(lambda: rise(half).start())
+        pl.when(jnp.logical_not(lifts))(
+            lambda: pltpu.make_async_copy(buf.at[0, r, half], middle.at[half], rrecv.at[half]).start()
+        )
+
     gather = TorusGather(x, y, panel_view, sends, recvs)
     gather.start()
 
-    def z_copy(block, half, target, n, k):
+    def ring_copy(offset, half, target, send, recv):
+        ref = buf.at[1, ((z + offset + 8) % 8) * 2 + c, half]
         return pltpu.make_async_remote_copy(
-            src_ref=buf.at[jnp.where(root, 0, 1), block, half],
-            dst_ref=buf.at[1, block, half],
-            send_sem=zsends.at[n, k],
-            recv_sem=zrecvs.at[n, half],
-            device_id=target,
-            device_id_type=MESH,
-        )
-
-    def z_wait(block, half, n):
-        ref = buf.at[1, block, half]
-        pltpu.make_async_copy(ref, ref, zrecvs.at[n, half]).wait()
-
-    hops = jnp.where(c == 0, dz, (8 - dz) % 8)
-    not_end = hops != 7
-
-    def pass_on(n):
-        @pl.when(root)
-        def _():
-            for half in (0, 1):
-                block = block_of(x, y, half, n)
-                z_copy(block, half, up if half == 0 else down, n, half).start()
-                z_copy(block, half, other, n, half + 2).start()
-
-        for half in (0, 1):
-            @pl.when(jnp.logical_and(jnp.logical_not(root_chip), c == half))
-            def _():
-                block = block_of(x, y, half, n)
-                z_wait(block, half, n)
-
-                @pl.when(not_end)
-                def _():
-                    z_copy(block, half, up if half == 0 else down, n, 0).start()
-
-                z_copy(block, half, other, n, 1).start()
-
-    def drained(n):
-        ref = buf.at[0, 0, 0]
-
-        @pl.when(root)
-        def _():
-            for k in range(4):
-                pltpu.make_async_copy(ref, ref, zsends.at[n, k]).wait()
-
-        @pl.when(jnp.logical_not(root_chip))
-        def _():
-            @pl.when(not_end)
-            def _():
-                pltpu.make_async_copy(ref, ref, zsends.at[n, 0]).wait()
-
-            pltpu.make_async_copy(ref, ref, zsends.at[n, 1]).wait()
-
-    from_root = jnp.where(root, 0, 1)
-
-    def decode(half, u):
+            src_ref=ref, dst_ref=ref, send_sem=send, recv_sem=recv, device_id=target, device_id_type=MESH
+        )
+
+    def half_wait(owner, half, sem):
+        ref = buf.at[1, owner, half]
+        pltpu.make_async_copy(ref, ref, sem).wait()
+
+    def ring_step(k):
+        for half in (0, 1):
+            for d, side in ((1, 0), (-1, 1)):
+                if k == 4 and half != side:
+                    continue
+                if k == 0:
+                    if d == 1:
+                        half_wait(p, half, trecv.at[half])
+                else:
+                    half_wait(((z - d * k + 8) % 8) * 2 + c, half, zrecv.at[side, k - 1, half])
+                if k < 3 or (k == 3 and half == side):
+                    ring_copy(-d * k, half, along[d], zsend.at[side, k, half], zrecv.at[side, k, half]).start()
+                if k > 0 or d == 1:
+                    o = (8 - d * k) % 8
+                    ring_copy(o, half, other, zsend2.at[o, half], zrecv2.at[o, half]).start()
+
+    def compute(o):
+        zz = (z + o + 8) % 8
+        for half in (0, 1):
+            half_wait(2 * zz + 1 - c, half, zrecv2.at[(o + 8) % 8, half])
         for v in (0, 1):
-            blocks = [block_of(x, y, half, 4 * u + 2 * v + k) for k in (0, 1)]
-
-            @pl.when(jnp.logical_and(jnp.logical_not(root), jnp.logical_or(root_chip, c != half)))
-            def _():
-                for k in (0, 1):
-                    z_wait(blocks[k], half, 4 * u + 2 * v + k)
-
-            scale_p = [column_scale(buf[0, b, half, pl.ds(512, 16), :], 2.0 ** -11) for b in blocks]
-            scale_r = [column_scale(buf[from_root, b, half, pl.ds(512, 16), :], 1.0) for b in blocks]
+            b, slot = (7 * r + 32 - 2 * zz - v) % 16, 2 * zz + v
+            scale_p = column_scale(buf[0, b, 0, pl.ds(512, 16), :], 2.0 ** -11)
+            scale_r = column_scale(buf[1, slot, 0, pl.ds(512, 16), :], 1.0)
+            spot = pl.ds(v * 128, 128)
             for j in range(8):
                 span = slice(128 * j, 128 * j + 128)
-                piece = pl.ds(64 * j, 64)
-                both_p = jnp.concatenate([
-                    buf[0, b, half, piece, :].astype(jnp.int32).astype(f32) * scale[j : j + 1, :]
-                    for b, scale in zip(blocks, scale_p)
-                ], axis=0)
-                spot = pl.ds(v * 128, 128)
-                hp[half, spot, span], lp[half, spot, span] = split_bf16(both_p)
-                both_r = jnp.concatenate([
-                    buf[from_root, b, half, piece, :].astype(jnp.int32).astype(f32) * scale[j : j + 1, :]
-                    for b, scale in zip(blocks, scale_r)
-                ], axis=0)
-                hrt[half, span, spot], lrt[half, span, spot] = split_bf16(both_r.T)
-
-    def multiply(half, t):
-        span = pl.ds(pl.multiple_of(t * 256, 256), 256)
-        high = hrt[half]
-        left = jnp.concatenate([high, high, lrt[half]], axis=1)
-        right_high = hp[half, :, span]
-        right = jnp.concatenate([right_high, lp[half, :, span], right_high], axis=0)
-        out_ref[:, span] += dot(left, right)
-
-    events = {
-        2: gather.first, 5: lambda: gather.across(0), 6: gather.far, 8: lambda: gather.across(1),
-        10: lambda: gather.across(-1), 12: lambda: gather.last(0), 13: lambda: gather.across(2),
-        15: lambda: gather.last(1), 16: lambda: gather.last(-1), 17: lambda: gather.last(2),
-    }
-
-    @pl.loop(FIRST_SLOT, FIRST_SLOT + 16 + 13 + 8)
-    def _(s):
-        for slot, event in events.items():
-            pl.when(s == slot)(event)
-        n = s - FIRST_SLOT - hop_slots(hops)
-
-        @pl.when(jnp.logical_and(n >= 0, n < 16))
-        def _():
-            pass_on(n)
-
-        @pl.loop(0, 2)
-        def _(half):
-            steps = hop_slots(jnp.where(half == 0, dz, (8 - dz) % 8))
-            late = jnp.where(jnp.logical_or(root, jnp.logical_and(half == c, jnp.logical_not(root_chip))), 0, 1)
-            m = s - FIRST_SLOT - steps - late - 3
-
-            @pl.when(jnp.logical_and(m >= 0, m < 16))
-            def _():
-                @pl.when(m % 4 == 0)
-                def _():
-                    decode(half, m // 4)
-
-                multiply(half, m % 4)
+                both = [
+                    jnp.concatenate([buf[k, at, half, pl.ds(64 * j, 64), :] for half in (0, 1)], axis=0)
+                    .astype(jnp.int32).astype(f32) * scale[j : j + 1, :]
+                    for k, at, scale in ((0, b, scale_p), (1, slot, scale_r))
+                ]
+                hp[spot, span], lp[spot, span] = split_bf16(both[0])
+                hrt[span, spot], lrt[span, spot] = split_bf16(both[1].T)
+
+        @pl.loop(0, 4)
+        def _(t):
+            span = pl.ds(pl.multiple_of(t * 256, 256), 256)
+            high = hrt[...]
+            left = jnp.concatenate([high, high, lrt[...]], axis=1)
+            right_high = hp[:, span]
+            right = jnp.concatenate([right_high, lp[:, span], right_high], axis=0)
+            out_ref[:, span] += dot(left, right)
+
+    gather.first()
+    for half in (0, 1):
+        pltpu.make_async_copy(middle.at[half], middle.at[half], rrecv.at[half]).wait()
+        pl.when(drops)(lambda: turn(half).start())
+        pl.when(jnp.logical_not(drops))(
+            lambda: pltpu.make_async_copy(middle.at[half], buf.at[1, p, half], trecv.at[half]).start()
+        )
+    gather.across(0)
+    gather.far()
+    ring_step(0)
+    gather.across(1)
+    gather.across(-1)
+    gather.last(0)
+    gather.across(2)
+    ring_step(1)
+    gather.last(1)
+    gather.last(-1)
+    gather.last(2)
+
+    @pl.loop(0, 2)
+    def _(i):
+        compute(i)
+
+    ring_step(2)
+
+    @pl.loop(0, 2)
+    def _(i):
+        compute(3 * i - 1)
+
+    ring_step(3)
+
+    @pl.loop(0, 3)
+    def _(i):
+        compute(jnp.where(i == 0, -2, 9 - 6 * i))
+
+    ring_step(4)
+    compute(4)
 
     spread.drain()
     gather.drain()
@@ -491,9 +462,17 @@
     for n in range(16):
         feat_wait(0, fsend.at[n], 0 if n in (9, 11) else None)
 
-    @pl.loop(0, 16)
-    def _(n):
-        drained(n)
+    for half in (0, 1):
+        pl.when(lifts)(lambda: rise(half).wait_send())
+        pl.when(drops)(lambda: turn(half).wait_send())
+
+    for half in (0, 1):
+        for side in (0, 1):
+            for k in range(4):
+                if k < 3 or half == side:
+                    half_wait(0, half, zsend.at[side, k, half])
+        for o in range(8):
+            half_wait(0, half, zsend2.at[o, half])
 
 
 def on_device(env_desc, point_desc, pool_index, pool_count, pool_weight, row_dest):
@@ -511,12 +490,13 @@
             VMEM((128, 128), f32),
             VMEM((512, 1024), bf16),
             VMEM((2, 16, 2, HALF, 128), i16),
-            VMEM((2, 256, 1024), bf16),
-            VMEM((2, 256, 1024), bf16),
-            VMEM((2, 1024, 256), bf16),
-            VMEM((2, 1024, 256), bf16),
+            VMEM((256, 1024), bf16),
+            VMEM((256, 1024), bf16),
+            VMEM((1024, 256), bf16),
+            VMEM((1024, 256), bf16),
             sem((40,)), sem((40,)), sem((15,)), sem((15,)), sem(()), sem((16,)), sem((8,)), sem((8,)),
-            sem((40,)), sem((40,)), sem((16, 4)), sem((16, 2)),
+            sem((40,)), sem((40,)), VMEM((2, HALF, 128), i16),
+            sem((2,)), sem((2,)), sem((2,)), sem((2,)), sem((2, 4, 2)), sem((2, 4, 2)), sem((8, 2)), sem((8, 2)),
         ],
         compiler_params=pltpu.CompilerParams(collective_id=1, has_side_effects=True, vmem_limit_bytes=56 << 20),
         name="whole",

time: 113 us -> 99.6 us (0.88)
  the two profiles are of different devices: /device:TPU:35 before, /device:TPU:1 now
where the time goes in v4:
time: 99.6 us; the launch traced here: 99.5 us
  Pallas kernels  96 us (96%)
  local copies, waits for them, and re-layouts  2.81 us (3%)
    pallas_call x1, Pallas kernels, on_device(): pl.pallas_call(whole_kernel, out_shape=(pltpu.VMEM((128, 1024), f32), plt...  96 us
    unnamed x2, local copies, waits for them, and re-layouts  2.81 us

profile of v4, /device:TPU:1, one launch (start us, length us, event | category | flops | bytes accessed | tf_op | source)
XLA Modules:
  0.0 99.5 jit_solution(3958030665406817221)
XLA Ops:
  0.6 96.0 %whole.1 = (f32[128,1024]{1,0:T(8,128)S(1)}, f32[1024,1024]{1,0:T(8,128)S(1)}) custom-call(bf16[64,512]{1,0:T(8,128)(2,1)} %bitcast.7, bf16[64,1024]{1,0:T(8,128)(2,1)} %bitcast.6, s32[4,256]{1,0:T(4,128)} %bitcast.8, s32[1,256]{1,0:T(1,128)} %bitcast.10, f32[4,256]{1,0:T(4,128)} %bitcast.9, s32[1,256]{1,0:T(1,128)} %bitcast.11), custom_call_target="tpu_custom_call" | custom-call | tf_op jit(solution)/shard_map/whole/pallas_call | solution.py:480
  96.7 0.8 copy.10
  97.5 2.0 %copy.11 = f32[1024,1024]{1,0:T(8,128)} copy(f32[1024,1024]{1,0:T(8,128)S(1)} %get-tuple-element.3) | data formatting | bytes 8388608

commit v5 on v4

--- a/solution.py
+++ b/solution.py
@@ -394,28 +394,38 @@
         for half in (0, 1):
             half_wait(2 * zz + 1 - c, half, zrecv2.at[(o + 8) % 8, half])
         for v in (0, 1):
-            b, slot = (7 * r + 32 - 2 * zz - v) % 16, 2 * zz + v
-            scale_p = column_scale(buf[0, b, 0, pl.ds(512, 16), :], 2.0 ** -11)
-            scale_r = column_scale(buf[1, slot, 0, pl.ds(512, 16), :], 1.0)
+            slot = 2 * zz + v
+            scale = column_scale(buf[1, slot, 0, pl.ds(512, 16), :], 1.0)
             spot = pl.ds(v * 128, 128)
             for j in range(8):
                 span = slice(128 * j, 128 * j + 128)
-                both = [
-                    jnp.concatenate([buf[k, at, half, pl.ds(64 * j, 64), :] for half in (0, 1)], axis=0)
-                    .astype(jnp.int32).astype(f32) * scale[j : j + 1, :]
-                    for k, at, scale in ((0, b, scale_p), (1, slot, scale_r))
-                ]
-                hp[spot, span], lp[spot, span] = split_bf16(both[0])
-                hrt[span, spot], lrt[span, spot] = split_bf16(both[1].T)
+                hrt[span, spot], lrt[span, spot] = split_bf16(both_halves(1, slot, j, scale).T)
+        first, second = (7 * r + 32 - 2 * zz) % 16, (7 * r + 31 - 2 * zz) % 16
 
         @pl.loop(0, 4)
         def _(t):
             span = pl.ds(pl.multiple_of(t * 256, 256), 256)
             high = hrt[...]
             left = jnp.concatenate([high, high, lrt[...]], axis=1)
-            right_high = hp[:, span]
-            right = jnp.concatenate([right_high, lp[:, span], right_high], axis=0)
+            right_high = jnp.concatenate([hp[first, :, span], hp[second, :, span]], axis=0)
+            right = jnp.concatenate([right_high, lp[first, :, span], lp[second, :, span], right_high], axis=0)
             out_ref[:, span] += dot(left, right)
+
+    def both_halves(k, at, j, scale):
+        parts = [buf[k, at, half, pl.ds(64 * j, 64), :] for half in (0, 1)]
+        return jnp.concatenate(parts, axis=0).astype(jnp.int32).astype(f32) * scale[j : j + 1, :]
+
+    def decode(steps):
+        packed = sum((4 * dx + dy) << (4 * i) for i, (dx, dy) in enumerate(steps))
+
+        @pl.loop(0, len(steps))
+        def _(i):
+            code = (jnp.int32(packed) >> (4 * i)) & 15
+            b = plane_id(x, y, code // 4, code % 4)
+            scale = column_scale(buf[0, b, 0, pl.ds(512, 16), :], 2.0 ** -11)
+            for j in range(8):
+                span = slice(128 * j, 128 * j + 128)
+                hp[b, :, span], lp[b, :, span] = split_bf16(both_halves(0, b, j, scale))
 
     gather.first()
     for half in (0, 1):
@@ -426,15 +436,18 @@
         )
     gather.across(0)
     gather.far()
+    decode([(0, 0), (1, 0), (3, 0), (0, 1), (0, 3)])
+    gather.across(1)
     ring_step(0)
-    gather.across(1)
     gather.across(-1)
     gather.last(0)
     gather.across(2)
+    decode([(1, 1), (1, 3), (3, 1), (3, 3), (2, 0), (0, 2)])
     ring_step(1)
     gather.last(1)
     gather.last(-1)
     gather.last(2)
+    decode([(2, 1), (2, 3), (1, 2), (3, 2), (2, 2)])
 
     @pl.loop(0, 2)
     def _(i):
@@ -490,8 +503,8 @@
             VMEM((128, 128), f32),
             VMEM((512, 1024), bf16),
             VMEM((2, 16, 2, HALF, 128), i16),
-            VMEM((256, 1024), bf16),
-            VMEM((256, 1024), bf16),
+            VMEM((16, 128, 1024), bf16),
+            VMEM((16, 128, 1024), bf16),
             VMEM((1024, 256), bf16),
             VMEM((1024, 256), bf16),
             sem((40,)), sem((40,)), sem((15,)), sem((15,)), sem(()), sem((16,)), sem((8,)), sem((8,)),

time: 99.6 us -> 98.3 us (0.987)
  Pallas kernels: 96 us -> 94.7 us
    pallas_call x1, Pallas kernels: 96 us -> 94.7 us  [on_device(): pl.pallas_call(whole_kernel, out_shape=(pltpu.VMEM((128, 1024), f32), plt...]
where the time goes in v5:
time: 98.3 us; the launch traced here: 98.2 us
  Pallas kernels  94.7 us (96%)
  local copies, waits for them, and re-layouts  2.81 us (3%)
    pallas_call x1, Pallas kernels, on_device(): pl.pallas_call(whole_kernel, out_shape=(pltpu.VMEM((128, 1024), f32), plt...  94.7 us
    unnamed x2, local copies, waits for them, and re-layouts  2.81 us

profile of v5, /device:TPU:1, one launch (start us, length us, event | category | flops | bytes accessed | tf_op | source)
XLA Modules:
  0.0 98.2 jit_solution(3687698741543019393)
XLA Ops:
  0.6 94.7 %whole.1 = (f32[128,1024]{1,0:T(8,128)S(1)}, f32[1024,1024]{1,0:T(8,128)S(1)}) custom-call(bf16[64,512]{1,0:T(8,128)(2,1)} %bitcast.7, bf16[64,1024]{1,0:T(8,128)(2,1)} %bitcast.6, s32[4,256]{1,0:T(4,128)} %bitcast.8, s32[1,256]{1,0:T(1,128)} %bitcast.10, f32[4,256]{1,0:T(4,128)} %bitcast.9, s32[1,256]{1,0:T(1,128)} %bitcast.11), custom_call_target="tpu_custom_call" | custom-call | tf_op jit(solution)/shard_map/whole/pallas_call | solution.py:493
  95.4 0.8 copy.10
  96.2 2.0 %copy.11 = f32[1024,1024]{1,0:T(8,128)} copy(f32[1024,1024]{1,0:T(8,128)S(1)} %get-tuple-element.3) | data formatting | bytes 8388608
